TPU v7x, 256 devices: a whole 4x4x8 slice. The times are simulated.
256 devices in a mesh: req: 8 (over z_lo, y), dev: 32 (over z_hi, x, core).
Axes of the slice: x: 4, y: 4, z: 8 (z_hi: 4, z_lo: 2; z = z_hi * 2 + z_lo), core: 2. Of those that a mesh axis runs over, the one named last changes fastest.
Arguments:
- hidden_in: bfloat16 [8, 1024, 2048], P('req', 'dev'), may hold values from -60 to 60
- attention_gain: float32 [2048], replicated, may hold values from 0.1 to 1.9
- query_weight: bfloat16 [2048, 2048], P('dev'), may hold values from -0.625 to 0.625
- keyval_weight: bfloat16 [1024, 2048], P('dev'), may hold values from -0.5 to 0.5
- out_weight: bfloat16 [2048, 2048], P('dev'), may hold values from -0.0625 to 0.0625
- feedforward_gain: float32 [2048], replicated, may hold values from 0.1 to 1.9
- gate_weight: bfloat16 [8192, 2048], P(('req', 'dev')), may hold values from -0.125 to 0.125
- up_weight: bfloat16 [8192, 2048], P(('req', 'dev')), may hold values from -0.125 to 0.125
- down_weight: bfloat16 [8192, 2048], P(('req', 'dev')), may hold values from -0.0625 to 0.0625
- prefix_pool: bfloat16 [8, 256, 16, 8, 128], P('req', 'dev'), may hold values from -640 to 640
- page_table: int32 [8, 256], P('req'), may hold values from 0 to 255, each once within a row
- prefix_length: int32 [8], P('req'), may hold values from 1 to 4096, 20480 in all
Outputs:
- hidden_out: bfloat16 [8, 1024, 2048], P('req', 'dev')
- new_keyval: bfloat16 [8, 1024, 8, 128], P('req', 'dev')
Inputs may be any that keep to these rules, and one draw needn't show every extreme that they name: `page_table`: each row names every page of the request's pool once. `prefix_length`: the longest cached prefix is exactly 4096.
All inputs are finite; a program needn't handle non-finite values. No bound on the sum of `prefix_length` on one device may be relied on, other than what follows from the above.
Results may differ from a plain program's by a relative error of at most 0.013.
The roundings to bfloat16 on the way count: a program that leaves them out, or rounds other values in their place, can miss the bound.
Values may be sent and summed in bfloat16 or wider, within the bound.
A program may use at most 64 MiB of HBM per device.

v0:
```python
import jax
import jax.numpy as jnp
from jax import lax
from jax.sharding import PartitionSpec as P

HQ = 32
KVH = 8
HD = 64
PAGE = 16
KBLOCK = 512


ROPE_BASE = 10000000.0
EPS = 1e-05
ATTENTION_SCALE = 0.015625
MASKED = -1e30


def root_norm(activations, norm_gain):
    widened = activations.astype(jnp.float32)
    inverse_rms = lax.rsqrt(jnp.mean(widened * widened, axis=-1, keepdims=True) + EPS)
    return (widened * inverse_rms * norm_gain).astype(jnp.bfloat16)


def rotate(vector, positions):
    half_width = vector.shape[-1] // 2
    frequency = ROPE_BASE ** (-jnp.arange(half_width, dtype=jnp.float32) / half_width)
    angles = positions.astype(jnp.float32)[:, None] * frequency[None, :]
    cosine = jnp.cos(angles)[:, None, :]
    sine_part = jnp.sin(angles)[:, None, :]
    leading = vector[..., :half_width]
    trailing = vector[..., half_width:]
    return jnp.concatenate(
        [leading * cosine - trailing * sine_part, trailing * cosine + leading * sine_part], axis=-1
    )


def transposed_product(left, right):
    return lax.dot_general(
        left, right, (((1,), (1,)), ((), ())), preferred_element_type=jnp.float32
    )


def attend_block(carried, queries, key_part, value_part, allowed):
    row_max, row_total, summed = carried
    scores = transposed_product(queries, key_part)
    scores = jnp.where(allowed, scores, MASKED)
    new_max = jnp.maximum(row_max, jnp.max(scores, axis=1))
    factor = jnp.exp(row_max - new_max)
    weights = jnp.where(allowed, jnp.exp(scores - new_max[:, None]), 0.0)
    new_total = row_total * factor + jnp.sum(weights, axis=1)
    summed = summed * factor[:, None] + jnp.dot(
        weights.astype(jnp.bfloat16), value_part, preferred_element_type=jnp.float32
    )
    return (new_max, new_total, summed)


def on_device(
    hidden_in,
    attention_gain,
    query_weight,
    keyval_weight,
    out_weight,
    feedforward_gain,
    gate_weight,
    up_weight,
    down_weight,
    prefix_pool,
    page_table,
    prefix_length,
):
    local_tokens = hidden_in.shape[1]
    device_count = lax.axis_size("dev")
    all_count = local_tokens * device_count
    heads_here = query_weight.shape[0] // HD
    group_size = HQ // KVH
    member = lax.axis_index("dev")
    length = prefix_length[0]
    own_tokens = hidden_in[0]
    all_tokens = lax.all_gather(own_tokens, "dev", axis=0, tiled=True)
    normed = root_norm(all_tokens, attention_gain)
    positions = length + jnp.arange(all_count, dtype=jnp.int32)
    raw_columns = transposed_product(keyval_weight, normed).astype(jnp.bfloat16)
    keyval_all = lax.all_gather(raw_columns, "dev", axis=0, tiled=True)
    own_rows = lax.dynamic_slice_in_dim(
        keyval_all, member * local_tokens, local_tokens, 1
    ).T.reshape(local_tokens, KVH, 2 * HD)
    own_positions = lax.dynamic_slice_in_dim(positions, member * local_tokens, local_tokens, 0)
    own_keys = rotate(own_rows[..., :HD].astype(jnp.float32), own_positions).astype(jnp.bfloat16)
    new_keyval = jnp.concatenate([own_keys, own_rows[..., HD:]], axis=-1)
    shared_head = member * heads_here // group_size
    head_pair = lax.dynamic_slice_in_dim(keyval_all, shared_head * 2 * HD, 2 * HD, 0).T
    fresh_keys = rotate(head_pair[:, None, :HD].astype(jnp.float32), positions)[:, 0, :].astype(
        jnp.bfloat16
    )
    fresh_values = head_pair[:, HD:]
    query_full = transposed_product(normed, query_weight).reshape(all_count, heads_here, HD)
    queries = (
        (rotate(query_full, positions) * ATTENTION_SCALE)
        .astype(jnp.bfloat16)
        .reshape(all_count * heads_here, HD)
    )
    local_pool = prefix_pool[0]
    wanted = jnp.arange(device_count, dtype=jnp.int32) * heads_here // group_size
    outgoing = jnp.take(local_pool, wanted, axis=2)
    incoming = lax.all_to_all(outgoing, "dev", split_axis=2, concat_axis=0, tiled=True)
    pool_head = incoming[:, :, 0, :]
    page_rows = page_table[0]
    block_pages = KBLOCK // PAGE
    query_rows = all_count * heads_here
    carried = (
        jnp.full((query_rows,), MASKED, jnp.float32),
        jnp.zeros((query_rows,), jnp.float32),
        jnp.zeros((query_rows, HD), jnp.float32),
    )

    def prefix_step(block_index, running):
        page_ids = lax.dynamic_slice_in_dim(page_rows, block_index * block_pages, block_pages, 0)
        stored = jnp.take(pool_head, page_ids, axis=0).reshape(KBLOCK, 2 * HD)
        slot_ids = block_index * KBLOCK + jnp.arange(KBLOCK, dtype=jnp.int32)
        allowed = (slot_ids < length)[None, :]
        return attend_block(running, queries, stored[:, :HD], stored[:, HD:], allowed)

    block_count = (length + KBLOCK - 1) // KBLOCK
    carried = lax.fori_loop(0, block_count, prefix_step, carried)
    query_token = jnp.arange(query_rows, dtype=jnp.int32) // heads_here
    causal = jnp.arange(all_count, dtype=jnp.int32)[None, :] <= query_token[:, None]
    row_max, row_total, summed = attend_block(carried, queries, fresh_keys, fresh_values, causal)
    attended = (summed / row_total[:, None]).astype(jnp.bfloat16)
    rows_in = attended
    attention_own = lax.psum_scatter(
        jnp.dot(rows_in, out_weight, preferred_element_type=jnp.float32).astype(jnp.bfloat16),
        "dev",
        scatter_dimension=0,
        tiled=True,
    ).astype(jnp.float32)
    residual = own_tokens.astype(jnp.float32) + attention_own
    mlp_rows = lax.all_gather(root_norm(residual, feedforward_gain), "dev", axis=0, tiled=True)
    fetched = (
        lax.all_gather(gate_weight, "req", axis=0, tiled=True),
        lax.all_gather(up_weight, "req", axis=0, tiled=True),
        lax.all_gather(down_weight, "req", axis=0, tiled=True),
    )
    gate_rows, up_rows, down_rows = fetched
    rows_in = mlp_rows
    gate_act = transposed_product(rows_in, gate_rows)
    up_act = transposed_product(rows_in, up_rows)
    activated = (jax.nn.silu(gate_act) * up_act).astype(jnp.bfloat16)
    feedforward_own = lax.psum_scatter(
        jnp.dot(activated, down_rows, preferred_element_type=jnp.float32).astype(jnp.bfloat16),
        "dev",
        scatter_dimension=0,
        tiled=True,
    ).astype(jnp.float32)
    hidden_out = (residual + feedforward_own).astype(jnp.bfloat16)
    return (hidden_out[None], new_keyval[None])


def solution(mesh):
    placed = (
        P("req", "dev", None),
        P(),
        P("dev", None),
        P("dev", None),
        P("dev", None),
        P(),
        P(("req", "dev"), None),
        P(("req", "dev"), None),
        P(("req", "dev"), None),
        P("req", "dev", None, None, None),
        P("req", None),
        P("req"),
    )
    return jax.shard_map(
        on_device,
        mesh=mesh,
        in_specs=placed,
        out_specs=(P("req", "dev", None), P("req", "dev", None, None)),
        check_vma=False,
    )
```

profile of v0, /device:TPU:8, one launch (start us, length us, event | category | flops | bytes accessed | tf_op | source)
XLA Modules:
  0.0 543.2 jit_solution(16338885161745345462)
XLA Ops:
  8.1 0.7 all-gather.18.cloned.1.call-update
  8.8 65.8 %all-gather.18.cloned.1.call-done = bf16[1,1024,2048]{2,1,0:T(8,128)(2,1)} async-done(((bf16[1,32,2048]{2,1,0:T(8,128)(2,1)}), bf16[1,1024,2048]{2,1,0:T(8,128)(2,1)}) %all-gather.18.cloned.1.call-update) | async-done | bytes 4194320 | tf_op jit(solution)/shard_map/all_gather | solution.py:80
  74.6 3.2 fusion.11
  77.9 0.2 copy-done.2
  78.1 2.1 fusion.34
  80.2 0.8 gather_fusion.1
  81.1 1.1 select_bitcast_fusion
  82.2 6.6 %all-to-all-start = ((bf16[8,16,32,128]{3,1,0,2:T(8,128)(2,1)}), bf16[8,16,32,128]{3,1,0,2:T(8,128)(2,1)S(1)}, u32[]{:S(2)}, u32[]{:S(2)}) async-start(bf16[8,16,32,128]{3,1,0,2:T(8,128)(2,1)} %select_bitcast_fusion), calls=%async_computation | async-start | bytes 2097152 | tf_op jit(solution)/shard_map/all_to_all | solution.py:106
  89.6 3.7 fusion.25
  93.3 55.0 %all-gather.8.cloned.1.call-done = bf16[1024,1024]{1,0:T(8,128)(2,1)} async-done(((bf16[32,1024]{1,0:T(8,128)(2,1)}), bf16[1024,1024]{1,0:T(8,128)(2,1)}) %all-gather.8.cloned.1.call-update) | async-done | bytes 2097168 | tf_op jit(solution)/shard_map/all_gather | solution.py:84
  148.3 1.0 dynamic-slice_bitcast_fusion
  149.3 0.6 fusion.66
  149.9 0.2 copy.19
  150.2 13.3 %while.14 = (s32[]{:T(128)}, f32[1024]{0:T(1024)S(1)}, f32[1024]{0:T(1024)S(1)}, f32[1024,64]{0,1:T(8,128)S(1)}, s32[]{:T(128)}, /*index=5*/s32[]{:T(128)}, s32[...) while((s32[]{:T(128)}, f32[1024]{0:T(1024)S(1)}, ...), condition=%wide.region_4.5_spmd, body=%wide.region_1.4_spmd.sunk | while | flops 139661504 | bytes 7807763 | solution.py:125
  150.2 0.7 add_compare_fusion.2
  151.0 0.1 broadcast_in_dim.163
  151.1 0.6 gather_fusion
  151.7 0.1 bitcast_select_fusion.2
  151.9 0.5 select_reduce_fusion.2
  152.3 0.5 fusion.105
  152.8 0.6 convolution_add_fusion.2
  153.5 0.7 add_compare_fusion.2
  154.4 0.1 broadcast_in_dim.163
  154.4 0.6 gather_fusion
  155.0 0.1 bitcast_select_fusion.2
  155.2 0.5 select_reduce_fusion.2
  155.7 0.5 fusion.105
  156.2 0.6 convolution_add_fusion.2
  156.9 0.7 add_compare_fusion.2
  157.8 0.6 gather_fusion
  158.4 0.1 bitcast_select_fusion.2
  158.5 0.5 select_reduce_fusion.2
  159.0 0.5 fusion.105
  159.5 0.6 convolution_add_fusion.2
  160.2 0.7 add_compare_fusion.2
  161.1 0.6 gather_fusion
  161.7 0.1 bitcast_select_fusion.2
  161.8 0.5 select_reduce_fusion.2
  162.3 0.5 fusion.105
  162.8 0.6 convolution_add_fusion.2
  163.5 0.8 fusion.15
  164.3 2.0 copy-done.1
  166.3 0.4 fusion.16
  166.7 5.8 %convolution_convert_fusion.1 = bf16[1024,2048]{1,0:T(8,128)(2,1)} fusion(bf16[64,2048]{1,0:T(8,128)(2,1)S(1)} %copy-done, f32[1024,1024]{0,1:T(8,128)} %copy-done.1, f32[1024]{0:T(1024)S(1)} %max.6, f32[1024,64]{0,1:T(8,128)S(1)} %get-tuple-element.52, bf16[1024,128]{0,1:T(8,128)(2,1)S(1)} %dynamic-slice_bitcast_fusion, f32[1024]{0:T(1024)S(1)} %get-tuple-element.95, ...), kind=kOutput, calls=%fused_computation.31 | convolution fusion | flops 410255360 | bytes 9056256 | tf_op jit(solution)/shard_map/dot_general | solution.py:132
  172.6 0.5 all-gather.12.cloned.1.call-update
  173.2 109.3 %reduce-scatter.3.cloned.1.call-done = bf16[32,2048]{1,0:T(8,128)(2,1)} async-done(((bf16[1024,2048]{1,0:T(8,128)(2,1)}), bf16[32,2048]{1,0:T(8,128)(2,1)}) %reduce-scatter.3.cloned.1.call-update) | async-done | bytes 131088 | tf_op jit(solution)/shard_map/reduce_scatter | solution.py:131
  282.6 1.1 multiply_reduce_fusion
  283.6 1.7 multiply_convert_fusion
  285.4 0.5 all-gather.14.cloned.1.call-update
  285.9 0.7 all-gather.16.cloned.1.call-update
  286.6 0.2 reduce-scatter.5.cloned.1.call-start
  286.9 56.0 %all-gather.10.cloned.1.call-done = bf16[1024,2048]{1,0:T(8,128)(2,1)} async-done(((bf16[32,2048]{1,0:T(8,128)(2,1)}), bf16[1024,2048]{1,0:T(8,128)(2,1)}) %all-gather.10.cloned.1.call-update) | async-done | bytes 4194320 | tf_op jit(solution)/shard_map/all_gather | solution.py:138
  342.9 3.8 fusion.87
  346.7 34.9 %all-gather.14.cloned.1.call-done = bf16[256,2048]{1,0:T(8,128)(2,1)} async-done(((bf16[32,2048]{1,0:T(8,128)(2,1)}), bf16[256,2048]{1,0:T(8,128)(2,1)}) %all-gather.14.cloned.1.call-update) | async-done | bytes 1048592 | tf_op jit(solution)/shard_map/all_gather | solution.py:141
  381.6 42.4 %all-gather.16.cloned.1.call-done = bf16[256,2048]{1,0:T(8,128)(2,1)} async-done(((bf16[32,2048]{1,0:T(8,128)(2,1)}), bf16[256,2048]{1,0:T(8,128)(2,1)}) %all-gather.16.cloned.1.call-update) | async-done | bytes 1048592 | tf_op jit(solution)/shard_map/all_gather | solution.py:142
  424.0 9.2 %convolution_convert_fusion = bf16[1024,2048]{1,0:T(8,128)(2,1)} fusion(bf16[256,2048]{1,0:T(8,128)(2,1)} %all-gather.16.cloned.1.call-done, bf16[1024,2048]{1,0:T(8,128)(2,1)} %all-gather.10.cloned.1.call-done, bf16[256,2048]{1,0:T(8,128)(2,1)} %all-gather.14.cloned.1.call-done, f32[1024,256]{1,0:T(8,128)S(1)} %fusion.87), kind=kOutput, calls=%fused_computation.30 | convolution fusion | flops 2151153664 | bytes 11534336 | tf_op jit(solution)/shard_map/dot_general | solution.py:150
  433.3 0.1 multiply_cosine_fusion.1
  433.4 1.1 constant_dynamic-slice_fusion
  434.5 0.1 copy.22
  434.7 0.1 copy.23
  434.8 0.1 subtract_convert_fusion
  434.9 0.7 maximum_bitcast_fusion.2
  435.7 98.5 %reduce-scatter.5.cloned.1.call-done = bf16[32,2048]{1,0:T(8,128)(2,1)} async-done(((bf16[1024,2048]{1,0:T(8,128)(2,1)}), bf16[32,2048]{1,0:T(8,128)(2,1)}) %reduce-scatter.5.cloned.1.call-update) | async-done | bytes 131088 | tf_op jit(solution)/shard_map/reduce_scatter | solution.py:149
  534.2 1.6 fusion.69
  (78 shorter events, 1.6 us)
Async XLA Ops:
  8.0 158.7 %copy-start = (bf16[64,2048]{1,0:T(8,128)(2,1)S(1)}, bf16[64,2048]{1,0:T(8,128)(2,1)}, u32[]{:S(2)}) copy-start(bf16[64,2048]{1,0:T(8,128)(2,1)} %param.18) | copy-start | bytes 786436
  8.0 69.8 %copy-start.10 = (f32[2048]{0:T(1024)S(1)}, f32[2048]{0:T(1024)}, u32[]{:S(2)}) copy-start(f32[2048]{0:T(1024)} %param.15) | copy-start | bytes 24580
  8.0 69.8 %copy-start.9 = (bf16[32,2048]{1,0:T(8,128)(2,1)S(1)}, bf16[32,2048]{1,0:T(8,128)(2,1)}, u32[]{:S(2)}) copy-start(bf16[32,2048]{1,0:T(8,128)(2,1)} %param.17) | copy-start | bytes 393220
  8.0 66.6 %all-gather.18.cloned.1.call-start = ((), (), s32[]{:S(2)}) async-start(), calls=%async_computation.10 | async-start | bytes 4325376 | tf_op jit(solution)/shard_map/all_gather | solution.py:80
  8.8 139.5 %all-gather.8.cloned.1.call-start = ((), (), s32[]{:S(2)}) async-start(), calls=%async_computation.3 | async-start | bytes 2162688 | tf_op jit(solution)/shard_map/all_gather | solution.py:84
  74.6 3.4 copy-start.2
  78.1 2.1 copy-start.5
  80.1 9.5 %copy-start.8 = (bf16[64,2048]{1,0:T(8,128)(2,1)S(1)}, bf16[64,2048]{1,0:T(8,128)(2,1)}, u32[]{:S(2)}) copy-start(bf16[64,2048]{1,0:T(8,128)(2,1)} %param.16) | copy-start | bytes 786436
  82.2 67.9 %all-to-all-start = ((bf16[8,16,32,128]{3,1,0,2:T(8,128)(2,1)}), bf16[8,16,32,128]{3,1,0,2:T(8,128)(2,1)S(1)}, u32[]{:S(2)}, u32[]{:S(2)}) async-start(bf16[8,16,32,128]{3,1,0,2:T(8,128)(2,1)} %select_bitcast_fusion), calls=%async_computation | async-start | bytes 2097152 | tf_op jit(solution)/shard_map/all_to_all | solution.py:106
  88.8 193.7 %reduce-scatter.3.cloned.1.call-start = ((), (), s32[]{:S(2)}) async-start(), calls=%async_computation.4 | async-start | bytes 4325376 | tf_op jit(solution)/shard_map/reduce_scatter | solution.py:131
  89.6 60.5 %copy-start.7 = (s32[1,256]{1,0:T(1,128)S(1)}, s32[1,256]{1,0:T(1,128)}, u32[]{:S(2)}) copy-start(s32[1,256]{1,0:T(1,128)} %param.24) | copy-start | bytes 3076
  164.3 2.0 copy-start.1
  172.5 110.0 %copy-start.3 = (bf16[1,32,2048]{2,1,0:T(8,128)(2,1)S(1)}, bf16[1,32,2048]{2,1,0:T(8,128)(2,1)}, u32[]{:S(2)}) copy-start(bf16[1,32,2048]{2,1,0:T(8,128)(2,1)} %param.14) | copy-start | bytes 393220
  172.6 111.1 %copy-start.6 = (f32[2048]{0:T(1024)S(1)}, f32[2048]{0:T(1024)}, u32[]{:S(2)}) copy-start(f32[2048]{0:T(1024)} %param.19) | copy-start | bytes 24580
  172.6 114.3 %all-gather.12.cloned.1.call-start = ((), (), s32[]{:S(2)}) async-start(), calls=%async_computation.6 | async-start | bytes 1179648 | tf_op jit(solution)/shard_map/all_gather | solution.py:140
  173.2 169.8 %all-gather.10.cloned.1.call-start = ((), (), s32[]{:S(2)}) async-start(), calls=%async_computation.5 | async-start | bytes 4325376 | tf_op jit(solution)/shard_map/all_gather | solution.py:138
  285.3 96.3 %all-gather.14.cloned.1.call-start = ((), (), s32[]{:S(2)}) async-start(), calls=%async_computation.7 | async-start | bytes 1179648 | tf_op jit(solution)/shard_map/all_gather | solution.py:141
  285.9 138.1 %all-gather.16.cloned.1.call-start = ((), (), s32[]{:S(2)}) async-start(), calls=%async_computation.8 | async-start | bytes 1179648 | tf_op jit(solution)/shard_map/all_gather | solution.py:142
  286.6 247.6 %reduce-scatter.5.cloned.1.call-start = ((), (), s32[]{:S(2)}) async-start(), calls=%async_computation.9 | async-start | bytes 4325376 | tf_op jit(solution)/shard_map/reduce_scatter | solution.py:149
  433.2 101.1 %copy-start.4 = (bf16[32,2048]{1,0:T(8,128)(2,1)S(1)}, bf16[32,2048]{1,0:T(8,128)(2,1)}, u32[]{:S(2)}) copy-start(bf16[32,2048]{1,0:T(8,128)(2,1)} %reduce-scatter.3.cloned.1.call-done) | copy-start | bytes 393220
Sparse Core Ops, SparseCore 0:
  11.4 63.1 all-gather.17
  80.3 67.9 all-gather.7
  172.7 109.8 reduce-scatter.2
Sparse Core Ops, SparseCore 1:
  174.8 49.1 all-gather.11
  285.4 57.5 all-gather.9
  344.6 37.0 all-gather.13
  383.4 40.5 all-gather.15
  433.3 100.9 reduce-scatter.4
where the time goes:
time: 544 us; the launch traced here: 543 us
  waiting for transfers between devices  464 us (85%)
  matrix products  29.7 us (5%)
  between operations  16.5 us (3%)
  other arithmetic  16.4 us (3%)
  local copies, waits for them, and re-layouts  8.66 us (2%)
  starting transfers between devices  7.14 us (1%)
    reduce_scatter x1, waiting for transfers between devices, on_device(): lax.psum_scatter(jnp.dot(rows_in, out_weight, preferred_element_type=jnp....  109 us
    reduce_scatter x1, waiting for transfers between devices, on_device(): lax.psum_scatter(jnp.dot(activated, down_rows, preferred_element_type=jnp...  98.5 us
    all_gather x1, waiting for transfers between devices, on_device(): all_tokens = lax.all_gather(own_tokens, 'dev', axis=0, tiled=True)  65.8 us
    all_gather x1, waiting for transfers between devices, on_device(): lax.all_gather(root_norm(residual, feedforward_gain), 'dev', axis=0, tile...  56 us
    all_gather x1, waiting for transfers between devices, on_device(): keyval_all = lax.all_gather(raw_columns, 'dev', axis=0, tiled=True)  55 us
    all_gather x1, waiting for transfers between devices, on_device(): lax.all_gather(down_weight, 'req', axis=0, tiled=True)  42.4 us
    all_gather x1, waiting for transfers between devices, on_device(): lax.all_gather(up_weight, 'req', axis=0, tiled=True)  34.9 us
    dot_general x8, matrix products, transposed_product(): lax.dot_general(left, right, (((1,), (1,)), ((), ())), preferred_element_...  12.1 us
  transfers between devices with their start and end apart: 9, of which 7 were waited for; matrix products, arithmetic and copies ran while one was open for 3% of the time, Pallas kernels for 0%

commit v1 on v0

v1 whole, which is shorter than its diff:
```python
import jax
import jax.numpy as jnp
from jax import lax
from jax.experimental import pallas as pl
from jax.experimental.pallas import tpu as pltpu
from jax.sharding import PartitionSpec as P

MESH = pl.DeviceIdType.MESH
HQ = 32
KVH = 8
HD = 64
PAGE = 16
ROPE_BASE = 10000000.0
EPS = 1e-05
ATTENTION_SCALE = 0.015625
MASKED = -1e30
BF = jnp.bfloat16
F32 = jnp.float32
QT = 256
KC = 512


def root_norm(activations, norm_gain):
    widened = activations.astype(F32)
    inverse_rms = lax.rsqrt(jnp.mean(widened * widened, axis=-1, keepdims=True) + EPS)
    return (widened * inverse_rms * norm_gain).astype(BF)


def transposed_product(left, right):
    return lax.dot_general(left, right, (((1,), (1,)), ((), ())), preferred_element_type=F32)


def dev_of(zh, x, c):
    return (zh * 4 + x) * 2 + c


def place():
    d = lax.axis_index("dev")
    return d // 8, (d // 2) % 4, d % 2


class Links:
    def __init__(self, send_sems, recv_sems):
        self.send_sems, self.recv_sems = send_sems, recv_sems
        self.copies = []

    def make(self, i, src, dst, to):
        return pltpu.make_async_remote_copy(
            src_ref=src,
            dst_ref=dst,
            send_sem=self.send_sems.at[i],
            recv_sem=self.recv_sems.at[i],
            device_id=to,
            device_id_type=MESH,
        )

    def send(self, src, dst, to):
        i = len(self.copies)
        copy = self.make(i, src, dst, to)
        copy.start()
        self.copies.append(copy)
        return i, to

    def recv(self, handle, region):
        i, to = handle
        self.make(i, region, region, to).wait_recv()

    def drain(self):
        for copy in self.copies:
            copy.wait_send()


class Locals:
    def __init__(self, sems):
        self.sems, self.copies = sems, []

    def copy(self, src, dst):
        copy = pltpu.make_async_copy(src, dst, self.sems.at[len(self.copies)])
        copy.start()
        self.copies.append(copy)
        return copy


def greet(partners):
    barrier = pltpu.get_barrier_semaphore()
    for partner in partners:
        pl.semaphore_signal(barrier, inc=1, device_id=partner, device_id_type=MESH)
    pl.semaphore_wait(barrier, len(partners))


def halves(ref, i):
    rows = ref.shape[1] // 2
    return [ref.at[i, pl.ds(0, rows)], ref.at[i, pl.ds(rows, rows)]]


class Gather:
    def __init__(self, links, own, out):
        self.l, self.own, self.out = links, own, out
        zh, x, c = place()
        self.zh, self.x, self.c = zh, x, c
        self.zs = [{"dev": dev_of((zh + s) % 4, x, c)} for s in (1, 3)]
        self.xs = [{"dev": dev_of(zh, (x + s) % 4, c)} for s in (1, 3)]
        self.mate = {"dev": dev_of(zh, x, 1 - c)}
        self.waits = []

    def id(self, dz, dx, other=False):
        c = 1 - self.c if other else self.c
        return dev_of((self.zh + dz) % 4, (self.x + dx) % 4, c)

    def blk(self, dz, dx, other=False):
        return self.out.at[self.id(dz, dx, other)]

    def core(self, dz, dx, half=None):
        if half is None:
            here, there = self.blk(dz, dx), self.blk(dz, dx, True)
        else:
            here = halves(self.out, self.id(dz, dx))[half]
            there = halves(self.out, self.id(dz, dx, True))[half]
        self.waits.append((self.l.send(here, here, self.mate), there))

    def both_x(self, src, dst):
        return [self.l.send(src, dst, self.xs[0]), self.l.send(src, dst, self.xs[1])]

    def start(self):
        own, mine = self.own, self.blk(0, 0)
        self.z = [self.l.send(own, mine, self.zs[0]), self.l.send(own, mine, self.zs[1])]
        self.xh = {0: self.both_x(own, mine)}
        self.waits.append((self.l.send(own, mine, self.mate), self.blk(0, 0, True)))

    def z_near(self):
        self.zfar = []
        for s, dz in ((0, 3), (1, 1)):
            self.l.recv(self.z[s], self.blk(dz, 0))
            piece = halves(self.out, self.id(dz, 0))[s]
            self.zfar.append(self.l.send(piece, piece, self.zs[s]))
            self.xh[dz] = self.both_x(self.blk(dz, 0), self.blk(dz, 0))
            self.core(dz, 0)

    def x_near(self, dz):
        self.xfar = getattr(self, "xfar", {})
        self.xfar[dz] = []
        for s, dx in ((0, 3), (1, 1)):
            self.l.recv(self.xh[dz][s], self.blk(dz, dx))
            piece = halves(self.out, self.id(dz, dx))[s]
            self.xfar[dz].append(self.l.send(piece, piece, self.xs[s]))
            self.core(dz, dx)

    def z_far(self):
        self.xh2 = []
        for s in (0, 1):
            piece = halves(self.out, self.id(2, 0))[s]
            self.l.recv(self.zfar[s], piece)
            self.xh2.append(self.both_x(piece, piece))
        self.core(2, 0)

    def x_near_far(self):
        self.xfar[2] = []
        for s, dx in ((0, 3), (1, 1)):
            pieces = halves(self.out, self.id(2, dx))
            self.l.recv(self.xh2[s][s], pieces[s])
            self.xfar[2].append(self.l.send(pieces[s], pieces[s], self.xs[s]))
        for s, dx in ((0, 3), (1, 1)):
            pieces = halves(self.out, self.id(2, dx))
            self.l.recv(self.xh2[1 - s][s], pieces[1 - s])
            self.core(2, dx)

    def x_far(self, dz):
        pieces = halves(self.out, self.id(dz, 2))
        for s in (0, 1):
            self.l.recv(self.xfar[dz][s], pieces[s])
        self.core(dz, 2)

    def finish(self):
        for handle, region in self.waits:
            self.l.recv(handle, region)


GATHER_COPIES = 48


class ReqGather:
    def __init__(self, links, own, out):
        self.l, self.own, self.out = links, own, out
        r = lax.axis_index("req")
        self.zl, self.y = r // 4, r % 4
        self.zm = {"req": (1 - self.zl) * 4 + self.y}
        self.ys = [{"req": self.zl * 4 + (self.y + s) % 4} for s in (1, 3)]

    def id(self, other, dy):
        zl = 1 - self.zl if other else self.zl
        return zl * 4 + (self.y + dy) % 4

    def start(self):
        mine = self.out.at[self.id(False, 0)]
        self.zh = self.l.send(self.own, mine, self.zm)
        self.yh = [[self.l.send(self.own, mine, to) for to in self.ys]]

    def second(self):
        block = self.out.at[self.id(True, 0)]
        self.l.recv(self.zh, block)
        self.yh.append([self.l.send(block, block, to) for to in self.ys])

    def forward(self, other):
        self.fh = getattr(self, "fh", [])
        self.fh.append([])
        for s, dy in ((0, 3), (1, 1)):
            i = self.id(other, dy)
            self.l.recv(self.yh[other][s], self.out.at[i])
            piece = halves(self.out, i)[s]
            self.fh[other].append(self.l.send(piece, piece, self.ys[s]))

    def finish(self):
        for other in (0, 1):
            for s in (0, 1):
                self.l.recv(self.fh[other][s], halves(self.out, self.id(other, 2))[s])


def gather_kernel(
    hid, pool, wkv, gate, up, down,
    hid_all, kv_all, wkv_all, gate_all, up_all, down_all,
    pz, send_sems, recv_sems, local_sems,
):
    zh, x, c = place()
    r = lax.axis_index("req")
    links, local = Links(send_sems, recv_sems), Locals(local_sems)
    ag = Gather(links, hid, hid_all)
    mate_x, cross = {"dev": dev_of(zh, x + 1 - 2 * (x % 2), c)}, {"dev": dev_of(zh, 3 - x, c)}
    zfar = {"dev": dev_of((zh + 2) % 4, x, c)}
    weights = [ReqGather(links, *pair) for pair in ((gate, gate_all), (up, up_all), (down, down_all))]
    greet(ag.zs + ag.xs + [ag.mate, zfar, weights[0].zm] + weights[0].ys)

    ag.start()
    zstage = []
    for dz, to in ((1, ag.zs[0]), (3, ag.zs[1]), (2, zfar)):
        row = (zh + dz) % 4
        zstage.append((links.send(pool.at[pl.ds(2 * row, 2)], pz.at[zh], to), pz.at[(zh + 4 - dz) % 4]))
    for w in weights:
        w.start()
    j = (x % 2) * 2 + c
    w_mate = links.send(wkv, wkv_all.at[j], mate_x)
    w_core = links.send(wkv, wkv_all.at[j], ag.mate)
    own_pages = local.copy(pool.at[pl.ds(2 * zh, 2)], pz.at[zh])
    local.copy(hid, hid_all.at[dev_of(zh, x, c)])
    local.copy(wkv, wkv_all.at[j])
    for own, out in ((gate, gate_all), (up, up_all), (down, down_all)):
        local.copy(own, out.at[r])

    ag.z_near()
    ag.x_near(0)
    weights[0].second()
    own_pages.wait()
    for handle, region in zstage:
        links.recv(handle, region)
    pair = x // 2
    mx = x + 1 - 2 * (x % 2)
    local.copy(pz.at[:, pair], kv_all.at[x * 2 + c])
    p_mate = links.send(pz.at[:, pair], kv_all.at[x * 2 + c], mate_x)
    p_cross = links.send(pz.at[:, 1 - pair], kv_all.at[x * 2 + c], cross)
    p_core = [(links.send(pz.at[:, pair], kv_all.at[x * 2 + c], ag.mate), x)]
    ag.z_far()
    ag.x_near(3)
    ag.x_near(1)
    weights[1].second()
    weights[2].second()
    links.recv(w_mate, wkv_all.at[(1 - x % 2) * 2 + c])
    w_fwd = links.send(wkv_all.at[(1 - x % 2) * 2 + c], wkv_all.at[(1 - x % 2) * 2 + c], ag.mate)
    links.recv(p_cross, kv_all.at[(3 - x) * 2 + c])
    got = kv_all.at[(3 - x) * 2 + c]
    p_fwd = links.send(got, got, mate_x)
    p_core.append((links.send(got, got, ag.mate), 3 - x))
    links.recv(p_mate, kv_all.at[mx * 2 + c])
    got = kv_all.at[mx * 2 + c]
    p_core.append((links.send(got, got, ag.mate), mx))
    weights[0].forward(0)
    weights[0].forward(1)
    ag.x_near_far()
    ag.x_far(0)
    weights[1].forward(0)
    weights[1].forward(1)
    ag.x_far(3)
    ag.x_far(1)
    links.recv(p_fwd, kv_all.at[(3 - mx) * 2 + c])
    got = kv_all.at[(3 - mx) * 2 + c]
    p_core.append((links.send(got, got, ag.mate), 3 - mx))
    weights[2].forward(0)
    weights[2].forward(1)
    ag.x_far(2)
    links.recv(w_core, wkv_all.at[(x % 2) * 2 + 1 - c])
    links.recv(w_fwd, wkv_all.at[(1 - x % 2) * 2 + 1 - c])
    for handle, xx in p_core:
        links.recv(handle, kv_all.at[xx * 2 + 1 - c])
    for w in weights:
        w.finish()
    ag.finish()
    for copy in local.copies[1:]:
        copy.wait()
    links.drain()


def attention_kernel(q_ref, kv_ref, fresh_ref, bias_ref, out_ref, s_ref):
    tile = pl.program_id(0)
    q = q_ref[...]
    prefix = kv_ref.shape[0]
    chunks = prefix // KC

    def lanes_max(running, scores):
        for k in range(scores.shape[1] // 128):
            running = jnp.maximum(running, scores[:, k * 128 : (k + 1) * 128])
        return running

    def score_prefix(i, running):
        at = pl.ds(pl.multiple_of(i * KC, KC), KC)
        scores = transposed_product(q, kv_ref[at, :]) + bias_ref[:, at]
        s_ref[:, at] = scores
        return lanes_max(running, scores)

    running = lax.fori_loop(0, chunks, score_prefix, jnp.full((QT, 128), MASKED, F32))
    row = lax.broadcasted_iota(jnp.int32, (QT, QT), 0)
    col = lax.broadcasted_iota(jnp.int32, (QT, QT), 1)

    def score_fresh(i, running):
        at = pl.ds(pl.multiple_of(i * QT, QT), QT)
        scores = transposed_product(q, fresh_ref[at, :])
        scores = jnp.where(col + i * QT <= row + tile * QT, scores, MASKED)
        s_ref[:, pl.ds(pl.multiple_of(prefix + i * QT, QT), QT)] = scores
        return lanes_max(running, scores)

    running = lax.fori_loop(0, tile + 1, score_fresh, running)
    top = jnp.max(running, axis=1, keepdims=True)

    def weigh(at, keys, carried):
        total, summed = carried
        weights = jnp.exp(s_ref[:, at] - top)
        for k in range(weights.shape[1] // 128):
            total = total + weights[:, k * 128 : (k + 1) * 128]
        summed = summed + jnp.dot(weights.astype(BF), keys, preferred_element_type=F32)
        return total, summed

    def weigh_prefix(i, carried):
        at = pl.ds(pl.multiple_of(i * KC, KC), KC)
        return weigh(at, kv_ref[at, :], carried)

    def weigh_fresh(i, carried):
        at = pl.ds(pl.multiple_of(prefix + i * QT, QT), QT)
        return weigh(at, fresh_ref[pl.ds(pl.multiple_of(i * QT, QT), QT), :], carried)

    carried = (jnp.zeros((QT, 128), F32), jnp.zeros((QT, 2 * HD), F32))
    carried = lax.fori_loop(0, chunks, weigh_prefix, carried)
    total, summed = lax.fori_loop(0, tile + 1, weigh_fresh, carried)
    out_ref[...] = (summed / jnp.sum(total, axis=1, keepdims=True)).astype(BF)


class Scatter:
    def __init__(self, links, part, rc, q, xh, xf, res, zhalf, zfull):
        self.l = links
        self.part, self.rc, self.q, self.xh, self.xf = part, rc, q, xh, xf
        self.res, self.zhalf, self.zfull = res, zhalf, zfull
        zh, x, c = place()
        self.zh, self.x, self.c = zh, x, c
        self.zs = [{"dev": dev_of((zh + s) % 4, x, c)} for s in (1, 3)]
        self.xs = [{"dev": dev_of(zh, (x + s) % 4, c)} for s in (1, 3)]
        self.mate = {"dev": dev_of(zh, x, 1 - c)}
        self.dz = (2, 1, 3, 0)
        self.dx = (2, 1, 3, 0)
        self.ch, self.x1, self.x2 = {}, {}, {}

    def row(self, i):
        return (self.zh + self.dz[i]) % 4

    def block(self, i, k, other=False):
        return dev_of(self.row(i), (self.x + self.dx[k]) % 4, 1 - self.c if other else self.c)

    def cores(self, i):
        self.ch[i] = [self.l.send(self.part.at[self.block(i, k, True)], self.rc.at[i * 4 + k], self.mate) for k in range(4)]

    def pair_sum(self, i, k):
        self.l.recv(self.ch[i][k], self.rc.at[i * 4 + k])
        return self.part[self.block(i, k)].astype(F32) + self.rc[i * 4 + k].astype(F32)

    def first(self, i):
        self.q[i * 3] = self.pair_sum(i, 0).astype(BF)
        pieces = halves(self.q, i * 3)
        self.x1[i] = [self.l.send(pieces[s], self.xh.at[i * 2 + s], self.xs[s]) for s in (0, 1)]

    def second(self, i):
        self.x2[i] = []
        for s in (0, 1):
            value = self.pair_sum(i, 1 + s)
            self.l.recv(self.x1[i][s], self.xh.at[i * 2 + s])
            arrived = self.xh[i * 2 + s].astype(F32)
            top = value[:16] + arrived if s == 0 else value[:16]
            low = value[16:] + arrived if s == 1 else value[16:]
            self.q[i * 3 + 1 + s, pl.ds(0, 16)] = top.astype(BF)
            self.q[i * 3 + 1 + s, pl.ds(16, 16)] = low.astype(BF)
            self.x2[i].append(self.l.send(self.q.at[i * 3 + 1 + s], self.xf.at[i * 2 + s], self.xs[s]))

    def row_sum(self, i):
        value = self.pair_sum(i, 3)
        for s in (0, 1):
            self.l.recv(self.x2[i][s], self.xf.at[i * 2 + s])
            value = value + self.xf[i * 2 + s].astype(F32)
        return value

    def third(self, i):
        value = self.row_sum(i)
        if i == 0:
            self.res[0] = value.astype(BF)
            pieces = halves(self.res, 0)
            self.z1 = [self.l.send(pieces[s], self.zhalf.at[s], self.zs[s]) for s in (0, 1)]
            self.z2 = [None, None]
            return None
        if i == 3:
            for s in (0, 1):
                self.l.recv(self.z2[s], self.zfull.at[s])
                value = value + self.zfull[s].astype(F32)
            return value
        s = i - 1
        self.l.recv(self.z1[s], self.zhalf.at[s])
        arrived = self.zhalf[s].astype(F32)
        top = value[:16] + arrived if s == 0 else value[:16]
        low = value[16:] + arrived if s == 1 else value[16:]
        self.res[i, pl.ds(0, 16)] = top.astype(BF)
        self.res[i, pl.ds(16, 16)] = low.astype(BF)
        self.z2[s] = self.l.send(self.res.at[i], self.zfull.at[s], self.zs[s])
        return None

    def run(self, produce):
        produce(self.row(0))
        self.cores(0)
        produce(self.row(1))
        self.cores(1)
        self.first(0)
        produce(self.row(2))
        self.cores(2)
        self.first(1)
        self.second(0)
        produce(self.row(3))
        self.cores(3)
        self.first(2)
        self.second(1)
        self.third(0)
        self.first(3)
        self.second(2)
        self.third(1)
        self.second(3)
        self.third(2)
        return self.third(3)


SCATTER_COPIES = 36


def scatter_scratch(width):
    return [
        pltpu.VMEM((32, 32, width), BF),
        pltpu.VMEM((16, 32, width), BF),
        pltpu.VMEM((12, 32, width), BF),
        pltpu.VMEM((8, 16, width), BF),
        pltpu.VMEM((8, 32, width), BF),
        pltpu.VMEM((3, 32, width), BF),
        pltpu.VMEM((2, 16, width), BF),
        pltpu.VMEM((2, 32, width), BF),
    ]


def tail_kernel(att, wo, fresh, hid, gain, gate, up, down, out, kv_out, *scratch):
    s1, s2 = scratch[:8], scratch[8:16]
    normed, rows, act, send_sems, recv_sems, local_sems = scratch[16:]
    zh, x, c = place()
    d = lax.axis_index("dev")
    width = wo.shape[1]
    links, local = Links(send_sems, recv_sems), Locals(local_sems)
    one, two = Scatter(links, *s1), Scatter(links, *s2)
    ag = Gather(links, normed, rows)
    peers = [{"dev": (d + 4 * m) % 32} for m in range(1, 8)]
    greet(peers + ag.xs + [ag.mate])

    kv_h = []
    for m in range(1, 8):
        to = (d + 4 * m) % 32
        src = fresh.at[pl.ds(pl.multiple_of(to * 32, 32), 32)]
        kv_h.append(links.send(src, kv_out.at[d // 4], peers[m - 1]))
    own_kv = local.copy(fresh.at[pl.ds(pl.multiple_of(d * 32, 32), 32)], kv_out.at[d // 4])

    def project(row):
        tokens = att[pl.ds(pl.multiple_of(row * 256, 256), 256), :]

        def columns(n, carry):
            at = pl.ds(pl.multiple_of(n * 512, 512), 512)
            term = jnp.dot(tokens, wo[:, at], preferred_element_type=F32).astype(BF)
            one.part[pl.ds(row * 8, 8), :, at] = term.reshape(8, 32, 512)
            return carry

        lax.fori_loop(0, width // 512, columns, 0)

    residual = one.run(project) + hid[...].astype(F32)
    normed[...] = root_norm(residual, gain[...])
    ag.start()
    own_rows = local.copy(normed, rows.at[d])
    ag.z_near()
    ag.x_near(0)
    ag.z_far()
    ag.x_near(3)
    ag.x_near(1)
    ag.x_near_far()
    ag.x_far(0)
    ag.x_far(3)
    ag.x_far(1)
    ag.x_far(2)
    ag.finish()
    own_rows.wait()

    def feed(row):
        tokens = rows[pl.ds(row * 8, 8)].reshape(256, width)
        gated = transposed_product(tokens, gate[...])
        raised = transposed_product(tokens, up[...])
        act[...] = (gated / (1.0 + jnp.exp(-gated)) * raised).astype(BF)

        def columns(n, carry):
            at = pl.ds(pl.multiple_of(n * 512, 512), 512)
            term = jnp.dot(act[...], down[:, at], preferred_element_type=F32).astype(BF)
            two.part[pl.ds(row * 8, 8), :, at] = term.reshape(8, 32, 512)
            return carry

        lax.fori_loop(0, width // 512, columns, 0)

    out[...] = (residual + two.run(feed)).astype(BF)
    for m in range(1, 8):
        links.recv(kv_h[m - 1], kv_out.at[((d + 32 - 4 * m) % 32) // 4])
    own_kv.wait()
    links.drain()


def vmem(count):
    return [pl.BlockSpec(memory_space=pltpu.VMEM)] * count


def on_device(
    hidden_in, attention_gain, query_weight, keyval_weight, out_weight, feedforward_gain,
    gate_weight, up_weight, down_weight, prefix_pool, page_table, prefix_length,
):
    width = hidden_in.shape[2]
    tokens = 1024
    member = lax.axis_index("dev")
    length = prefix_length[0]
    own_tokens = hidden_in[0]
    slots = prefix_pool.shape[1] * PAGE
    pool = prefix_pool[0].transpose(2, 0, 1, 3).reshape(KVH, slots, 2 * HD)
    count = 110
    hidden_all, kv_all, wkv_all, gate_all, up_all, down_all = pl.pallas_call(
        gather_kernel,
        out_shape=[
            jax.ShapeDtypeStruct((32, 32, width), BF),
            jax.ShapeDtypeStruct((8, 4, slots, 2 * HD), BF),
            jax.ShapeDtypeStruct((4, 32, width), BF),
            jax.ShapeDtypeStruct((8, 32, width), BF),
            jax.ShapeDtypeStruct((8, 32, width), BF),
            jax.ShapeDtypeStruct((8, 32, width), BF),
        ],
        in_specs=vmem(6),
        out_specs=vmem(6),
        scratch_shapes=[
            pltpu.VMEM((4, 2, slots, 2 * HD), BF),
            pltpu.SemaphoreType.DMA((count,)),
            pltpu.SemaphoreType.DMA((count,)),
            pltpu.SemaphoreType.DMA((8,)),
        ],
        compiler_params=pltpu.CompilerParams(collective_id=0, has_side_effects=True, vmem_limit_bytes=60 << 20),
        name="gathers",
    )(own_tokens, pool, keyval_weight, gate_weight, up_weight, down_weight)

    logical = jnp.sum(
        jnp.where(
            page_table[0][None, :] == jnp.arange(256, dtype=jnp.int32)[:, None],
            jnp.arange(256, dtype=jnp.int32)[None, :],
            0,
        ),
        axis=1,
    )
    slot = logical[:, None] * PAGE + jnp.arange(PAGE, dtype=jnp.int32)[None, :]
    bias = jnp.where(slot < length, 0.0, MASKED).astype(F32)
    bias = bias.reshape(4, 8, slots).transpose(1, 0, 2).reshape(1, 32 * slots)

    normed = root_norm(hidden_all.reshape(tokens, width), attention_gain)
    columns = jnp.concatenate([query_weight, wkv_all.reshape(4 * 32, width)], axis=0)
    projected = transposed_product(normed, columns)
    positions = (length + jnp.arange(tokens, dtype=jnp.int32)).astype(F32)
    half = HD // 2
    frequency = ROPE_BASE ** (-jnp.arange(half, dtype=F32) / half)
    angles = positions[:, None] * frequency[None, :]
    cosine, sine = jnp.cos(angles), jnp.sin(angles)

    def rotate(vector):
        leading, trailing = vector[:, :half], vector[:, half:]
        return jnp.concatenate([leading * cosine - trailing * sine, trailing * cosine + leading * sine], axis=-1)

    queries = (rotate(projected[:, :HD]) * ATTENTION_SCALE).astype(BF)
    queries = jnp.concatenate([queries, jnp.zeros_like(queries)], axis=1)
    raw = projected[:, HD:].astype(BF)
    fresh = jnp.concatenate([rotate(raw[:, :HD].astype(F32)).astype(BF), raw[:, HD:]], axis=1)

    whole = lambda shape: pl.BlockSpec(shape, lambda i: (0, 0))
    attended = pl.pallas_call(
        attention_kernel,
        out_shape=jax.ShapeDtypeStruct((tokens, 2 * HD), BF),
        grid=(tokens // QT,),
        in_specs=[
            pl.BlockSpec((QT, 2 * HD), lambda i: (i, 0)),
            whole((32 * slots, 2 * HD)),
            whole((tokens, 2 * HD)),
            whole((1, 32 * slots)),
        ],
        out_specs=pl.BlockSpec((QT, 2 * HD), lambda i: (i, 0)),
        scratch_shapes=[pltpu.VMEM((QT, 32 * slots + tokens), F32)],
        name="attention",
    )(queries, kv_all.reshape(32 * slots, 2 * HD), fresh, bias)
    attended = attended[:, HD:]

    copies = GATHER_COPIES + 2 * SCATTER_COPIES + 8
    hidden_out, kv_out = pl.pallas_call(
        tail_kernel,
        out_shape=[jax.ShapeDtypeStruct((32, width), BF), jax.ShapeDtypeStruct((8, 32, 2 * HD), BF)],
        in_specs=vmem(8),
        out_specs=vmem(2),
        scratch_shapes=scatter_scratch(width) + scatter_scratch(width) + [
            pltpu.VMEM((32, width), BF),
            pltpu.VMEM((32, 32, width), BF),
            pltpu.VMEM((256, 256), BF),
            pltpu.SemaphoreType.DMA((copies,)),
            pltpu.SemaphoreType.DMA((copies,)),
            pltpu.SemaphoreType.DMA((2,)),
        ],
        compiler_params=pltpu.CompilerParams(collective_id=1, has_side_effects=True, vmem_limit_bytes=60 << 20),
        name="tail",
    )(
        attended, out_weight, fresh, own_tokens, feedforward_gain.reshape(1, width),
        gate_all.reshape(256, width), up_all.reshape(256, width), down_all.reshape(256, width),
    )
    return hidden_out[None], kv_out.transpose(1, 0, 2)[None]


def solution(mesh):
    placed = (
        P("req", "dev", None),
        P(),
        P("dev", None),
        P("dev", None),
        P("dev", None),
        P(),
        P(("req", "dev"), None),
        P(("req", "dev"), None),
        P(("req", "dev"), None),
        P("req", "dev", None, None, None),
        P("req", None),
        P("req"),
    )
    return jax.shard_map(
        on_device,
        mesh=mesh,
        in_specs=placed,
        out_specs=(P("req", "dev", None), P("req", "dev", None, None)),
        check_vma=False,
    )
```

time: 544 us -> 188 us (0.35)
  waiting for transfers between devices: 464 us -> 0 us
  Pallas kernels: 0 us -> 165 us
  matrix products: 29.7 us -> 1.27 us
  between operations: 16.5 us -> 1.42 us
  starting transfers between devices: 7.14 us -> 0 us
  other arithmetic: 16.4 us -> 10.9 us
    all_gather x6 -> x0, waiting for transfers between devices: 254 us -> none  [the longest x1 65.8 us: on_device(): all_tokens = lax.all_gather(own_tokens, 'dev', axis=0, tiled=True)]
    reduce_scatter x2 -> x0, waiting for transfers between devices: 208 us -> none  [the longest x1 109 us: on_device(): lax.psum_scatter(jnp.dot(rows_in, out_weight, preferred_element_type=jnp....]
    pallas_call x0 -> x3, Pallas kernels: none -> 165 us  [the longest x1 88.1 us: on_device(): pl.pallas_call(tail_kernel, out_shape=[jax.ShapeDtypeStruct((32, width),...]
    dot_general x6 -> x0, matrix products: 17.5 us -> none  [the longest x1 9.16 us: on_device(): jnp.dot(activated, down_rows, preferred_element_type=jnp.float32)]
    dot_general x8 -> x1, matrix products: 12.1 us -> 1.27 us  [transposed_product(): lax.dot_general(left, right, (((1,), (1,)), ((), ())), preferred_element_...]
    all_to_all x1 -> x0, starting transfers between devices: 6.63 us -> none  [on_device(): lax.all_to_all(outgoing, 'dev', split_axis=2, concat_axis=0, tiled=True)]
  transfers between devices with their start and end apart: 9 -> 0, of which waited for: 7 -> 0; matrix products, arithmetic and copies ran while one was open for 3% -> 0% of each run, Pallas kernels for 0% -> 0%
where the time goes in v1:
time: 188 us; the launch traced here: 187 us
  Pallas kernels  165 us (88%)
  other arithmetic  10.9 us (6%)
  local copies, waits for them, and re-layouts  7.76 us (4%)
    pallas_call x1, Pallas kernels, on_device(): pl.pallas_call(tail_kernel, out_shape=[jax.ShapeDtypeStruct((32, width),...  88.1 us
    pallas_call x1, Pallas kernels, on_device(): pl.pallas_call(gather_kernel, out_shape=[jax.ShapeDtypeStruct((32, 32, wi...  54.8 us
    pallas_call x1, Pallas kernels, on_device(): pl.pallas_call(attention_kernel, out_shape=jax.ShapeDtypeStruct((tokens,...  22.4 us

profile of v1, /device:TPU:8, one launch (start us, length us, event | category | flops | bytes accessed | tf_op | source)
XLA Modules:
  0.0 186.6 jit_solution(364668594273036179)
XLA Ops:
  0.6 0.0 copy-start
  0.6 1.7 copy.31
  2.3 54.8 %gathers.1 = (bf16[32,32,2048]{2,1,0:T(8,128)(2,1)}, bf16[8,4,128,128]{3,2,1,0:T(8,128)(2,1)}, bf16[4,32,2048]{2,1,0:T(8,128)(2,1)}, bf16[8,32,2048]{2,1,0:T(8,1...) custom-call(bf16[32,2048]{1,0:T(8,128)(2,1)} %bitcast.38, bf16[8,128,128]{2,1,0:T(8,128)(2,1)} %bitcast.34, ...), custom_call_target="tpu_custom_call" | custom-call | tf_op jit(solution)/shard_map/gathers/pallas_call | solution.py:550
  57.1 3.1 %multiply_reduce_fusion = f32[32,32]{1,0:T(8,128)S(1)} fusion(bf16[32,32,2048]{2,1,0:T(8,128)(2,1)} %get-tuple-element.10), kind=kLoop, calls=%fused_computation.3 | loop fusion | flops 6290432 | bytes 4198400 | tf_op jit(solution)/shard_map/reduce_sum | solution.py:25
  60.2 0.1 rsqrt.12
  60.3 0.0 copy-done
  60.3 0.0 copy-start.2
  60.3 0.0 copy-start.3
  60.3 3.3 %fusion.1 = bf16[1024,2048]{1,0:T(8,128)(2,1)S(1)} fusion(f32[2048]{0:T(1024)S(1)} %copy-done, f32[1024]{0:T(1024)S(1)} %rsqrt.12, bf16[32,32,2048]{2,1,0:T(8,128)(2,1)} %get-tuple-element.10), kind=kLoop, calls=%fused_computation.2 | loop fusion | flops 8388608 | bytes 8400896 | tf_op jit(solution)/shard_map/convert_element_type | solution.py:26
  63.6 0.0 copy-done.2
  63.6 0.0 copy-done.3
  63.6 1.3 fusion.23
  64.9 0.0 copy-start.1
  64.9 0.1 slice_convert_fusion
  65.7 2.5 %fusion.17 = (bf16[1024,32]{1,0:T(8,128)(2,1)S(1)}, bf16[1024,32]{1,0:T(8,128)(2,1)S(1)}, f32[1024,32]{1,0:T(8,128)S(1)}, f32[1024,32]{1,0:T(8,128)S(1)}) fusion(f32[1024,64]{1,0:T(8,128)S(1)} %get-tuple-element.30, f32[1024]{0:T(1024)S(1)} %add_convert_fusion, f32[32]{0:T(128)S(1)} %multiply_power_fusion, f32[1024,192]{1,0:T(8,128)S(1)} %get-tuple-element.35), kind=kLoop, calls=%fused_computation.21 | loop fusion | flops 491520 | bytes 921728 | tf_op jit(solution)/shard_map/convert.1
  68.3 0.9 pad_maximum_fusion.fresh_ref.fresh
  69.2 0.2 fusion.20
  69.4 0.7 concatenate.17.q_ref
  70.2 0.0 copy-done.1
  70.2 0.1 select_reduce_fusion
  70.3 0.1 mul.97
  70.4 0.1 add.56
  70.5 0.1 add.57
  70.6 0.1 add.59
  70.7 0.6 fusion.21
  71.3 22.4 %attention.1 = bf16[1024,128]{1,0:T(8,128)(2,1)} custom-call(bf16[1024,128]{1,0:T(8,128)(2,1)} %concatenate.17.q_ref, bf16[4096,128]{1,0:T(8,128)(2,1)} %bitcast.33, bf16[1024,128]{1,0:T(8,128)(2,1)} %pad_maximum_fusion.fresh_ref.fresh, f32[1,4096]{1,0:T(1,128)} %bitcast.42), custom_call_target="tpu_custom_call" | custom-call | tf_op jit(solution)/shard_map/attention/pallas_call | solution.py:603
  93.7 1.8 slice.41.att
  95.5 88.1 %tail.1 = (bf16[32,2048]{1,0:T(8,128)(2,1)}, bf16[8,32,128]{2,1,0:T(8,128)(2,1)}) custom-call(bf16[1024,64]{1,0:T(8,128)(2,1)} %slice.41.att, bf16[64,2048]{1,0:T(8,128)(2,1)} %wo.1, bf16[1024,128]{1,0:T(8,128)(2,1)} %pad_maximum_fusion.fresh_ref.fresh, bf16[32,2048]{1,0:T(8,128)(2,1)} %bitcast.39, f32[1,2048]{1,0:T(1,128)} %bitcast.44, ...), custom_call_target="tpu_custom_call" | custom-call | tf_op jit(solution)/shard_map/tail/pallas_call | solution.py:620
  183.6 1.5 copy.37
  185.1 1.6 copy.41
  (6 shorter events, 0.0 us)
Async XLA Ops:
  0.6 59.7 %copy-start = (f32[2048]{0:T(1024)S(1)}, f32[2048]{0:T(1024)}, u32[]{:S(2)}) copy-start(f32[2048]{0:T(1024)} %param.13) | copy-start | bytes 24580
  60.3 3.3 %copy-start.2 = (bf16[4,32,2048]{2,1,0:T(8,128)(2,1)S(1)}, bf16[4,32,2048]{2,1,0:T(8,128)(2,1)}, u32[]{:S(2)}) copy-start(bf16[4,32,2048]{2,1,0:T(8,128)(2,1)} %get-tuple-element.11) | copy-start | bytes 1572868
  60.3 3.3 %copy-start.3 = (bf16[64,2048]{1,0:T(8,128)(2,1)S(1)}, bf16[64,2048]{1,0:T(8,128)(2,1)}, u32[]{:S(2)}) copy-start(bf16[64,2048]{1,0:T(8,128)(2,1)} %param.14) | copy-start | bytes 786436
  64.9 5.3 %copy-start.1 = (s32[1,256]{1,0:T(1,128)S(1)}, s32[1,256]{1,0:T(1,128)}, u32[]{:S(2)}) copy-start(s32[1,256]{1,0:T(1,128)} %param.22) | copy-start | bytes 3076

commit v2 on v0

v2 whole, which is shorter than its diff:
```python
import jax
import jax.numpy as jnp
from jax import lax
from jax.experimental import pallas as pl
from jax.experimental.pallas import tpu as pltpu
from jax.sharding import PartitionSpec as P

MESH = pl.DeviceIdType.MESH
HQ = 32
KVH = 8
HD = 64
PAGE = 16
ROPE_BASE = 10000000.0
EPS = 1e-05
ATTENTION_SCALE = 0.015625
MASKED = -1e30
BF = jnp.bfloat16
F32 = jnp.float32
QT = 256
KC = 1024


def root_norm(activations, norm_gain):
    widened = activations.astype(F32)
    inverse_rms = lax.rsqrt(jnp.mean(widened * widened, axis=-1, keepdims=True) + EPS)
    return (widened * inverse_rms * norm_gain).astype(BF)


def transposed_product(left, right):
    return lax.dot_general(left, right, (((1,), (1,)), ((), ())), preferred_element_type=F32)


def dev_of(zh, x, c):
    return (zh * 4 + x) * 2 + c


def place():
    d = lax.axis_index("dev")
    return d // 8, (d // 2) % 4, d % 2


class Links:
    def __init__(self, send_sems, recv_sems):
        self.send_sems, self.recv_sems = send_sems, recv_sems
        self.copies = []

    def make(self, i, src, dst, to):
        return pltpu.make_async_remote_copy(
            src_ref=src,
            dst_ref=dst,
            send_sem=self.send_sems.at[i],
            recv_sem=self.recv_sems.at[i],
            device_id=to,
            device_id_type=MESH,
        )

    def send(self, src, dst, to):
        i = len(self.copies)
        copy = self.make(i, src, dst, to)
        copy.start()
        self.copies.append(copy)
        return i, to

    def recv(self, handle, region):
        i, to = handle
        self.make(i, region, region, to).wait_recv()

    def drain(self):
        for copy in self.copies:
            copy.wait_send()


class Locals:
    def __init__(self, sems):
        self.sems, self.copies = sems, []

    def copy(self, src, dst):
        copy = pltpu.make_async_copy(src, dst, self.sems.at[len(self.copies)])
        copy.start()
        self.copies.append(copy)
        return copy


def greet(partners):
    barrier = pltpu.get_barrier_semaphore()
    for partner in partners:
        pl.semaphore_signal(barrier, inc=1, device_id=partner, device_id_type=MESH)
    pl.semaphore_wait(barrier, len(partners))


def halves(ref, i):
    rows = ref.shape[1] // 2
    return [ref.at[i, pl.ds(0, rows)], ref.at[i, pl.ds(rows, rows)]]


class Gather:
    def __init__(self, links, own, out):
        self.l, self.own, self.out = links, own, out
        zh, x, c = place()
        self.zh, self.x, self.c = zh, x, c
        self.zs = [{"dev": dev_of((zh + s) % 4, x, c)} for s in (1, 3)]
        self.xs = [{"dev": dev_of(zh, (x + s) % 4, c)} for s in (1, 3)]
        self.mate = {"dev": dev_of(zh, x, 1 - c)}
        self.waits = {0: [], 1: [], 2: [], 3: []}
        self.xfar, self.xh = {}, {}

    def id(self, dz, dx, other=False):
        c = 1 - self.c if other else self.c
        return dev_of((self.zh + dz) % 4, (self.x + dx) % 4, c)

    def blk(self, dz, dx, other=False):
        return self.out.at[self.id(dz, dx, other)]

    def core(self, dz, dx):
        here, there = self.blk(dz, dx), self.blk(dz, dx, True)
        self.waits[dz].append((self.l.send(here, here, self.mate), there))

    def both_x(self, src, dst):
        return [self.l.send(src, dst, self.xs[0]), self.l.send(src, dst, self.xs[1])]

    def start(self):
        own, mine = self.own, self.blk(0, 0)
        self.z = [self.l.send(own, mine, self.zs[0]), self.l.send(own, mine, self.zs[1])]
        self.xh[0] = self.both_x(own, mine)
        self.waits[0].append((self.l.send(own, mine, self.mate), self.blk(0, 0, True)))

    def z_near(self):
        self.zfar = []
        for s, dz in ((0, 3), (1, 1)):
            self.l.recv(self.z[s], self.blk(dz, 0))
            piece = halves(self.out, self.id(dz, 0))[s]
            self.zfar.append(self.l.send(piece, piece, self.zs[s]))
            self.xh[dz] = self.both_x(self.blk(dz, 0), self.blk(dz, 0))
            self.core(dz, 0)

    def x_near(self, dz):
        self.xfar[dz] = []
        for s, dx in ((0, 3), (1, 1)):
            self.l.recv(self.xh[dz][s], self.blk(dz, dx))
            piece = halves(self.out, self.id(dz, dx))[s]
            self.xfar[dz].append(self.l.send(piece, piece, self.xs[s]))
            self.core(dz, dx)

    def z_far(self):
        self.xh2 = []
        for s in (0, 1):
            piece = halves(self.out, self.id(2, 0))[s]
            self.l.recv(self.zfar[s], piece)
            self.xh2.append(self.both_x(piece, piece))
        self.core(2, 0)

    def x_near_far(self):
        self.xfar[2] = []
        for s, dx in ((0, 3), (1, 1)):
            pieces = halves(self.out, self.id(2, dx))
            self.l.recv(self.xh2[s][s], pieces[s])
            self.xfar[2].append(self.l.send(pieces[s], pieces[s], self.xs[s]))
        for s, dx in ((0, 3), (1, 1)):
            pieces = halves(self.out, self.id(2, dx))
            self.l.recv(self.xh2[1 - s][s], pieces[1 - s])
            self.core(2, dx)

    def x_far(self, dz):
        pieces = halves(self.out, self.id(dz, 2))
        for s in (0, 1):
            self.l.recv(self.xfar[dz][s], pieces[s])
        self.core(dz, 2)

    def ready(self, dz):
        for handle, region in self.waits[dz]:
            self.l.recv(handle, region)


class WeightGather:
    def __init__(self, links, owns, out):
        self.l, self.owns, self.out = links, owns, out
        zh, x, c = place()
        r = lax.axis_index("req")
        self.zh, self.zl, self.y = zh, r // 4, r % 4
        self.zs = [{"dev": dev_of((zh + s) % 4, x, c)} for s in (1, 3)]
        self.ys = [{"req": self.zl * 4 + (self.y + s) % 4} for s in (1, 3)]
        self.yh, self.yfar = {}, {}

    def id(self, dz, dy):
        return ((self.zh + dz) % 4) * 4 + (self.y + dy) % 4

    def blk(self, dz, dy):
        return self.out.at[:, self.id(dz, dy)]

    def half(self, dz, dy, s):
        return self.out.at[:, self.id(dz, dy), pl.ds(16 * s, 16)]

    def spread(self, targets):
        mine = self.id(0, 0)
        return [[self.l.send(own, self.out.at[a, mine], to) for a, own in enumerate(self.owns)] for to in targets]

    def start_y(self):
        self.yh[0] = self.spread(self.ys)

    def start_z(self):
        self.z = self.spread(self.zs)

    def both_y(self, ref):
        return [self.l.send(ref, ref, to) for to in self.ys]

    def y_own(self):
        self.yfar[0] = []
        for s, dy in ((0, 3), (1, 1)):
            for a in range(3):
                self.l.recv(self.yh[0][s][a], self.out.at[a, self.id(0, dy)])
            piece = self.half(0, dy, s)
            self.yfar[0].append(self.l.send(piece, piece, self.ys[s]))

    def z_near(self):
        self.zfar = []
        for s, dz in ((0, 3), (1, 1)):
            for a in range(3):
                self.l.recv(self.z[s][a], self.out.at[a, self.id(dz, 0)])
            piece = self.half(dz, 0, s)
            self.zfar.append(self.l.send(piece, piece, self.zs[s]))
            self.yh[dz] = self.both_y(self.blk(dz, 0))

    def z_far(self):
        self.yh2 = []
        for s in (0, 1):
            piece = self.half(2, 0, s)
            self.l.recv(self.zfar[s], piece)
            self.yh2.append(self.both_y(piece))

    def y_near(self, dz):
        self.yfar[dz] = []
        for s, dy in ((0, 3), (1, 1)):
            self.l.recv(self.yh[dz][s], self.blk(dz, dy))
            piece = self.half(dz, dy, s)
            self.yfar[dz].append(self.l.send(piece, piece, self.ys[s]))

    def y_near_far(self):
        self.yfar[2] = []
        for s, dy in ((0, 3), (1, 1)):
            piece = self.half(2, dy, s)
            self.l.recv(self.yh2[s][s], piece)
            self.yfar[2].append(self.l.send(piece, piece, self.ys[s]))
        for s, dy in ((0, 3), (1, 1)):
            self.l.recv(self.yh2[1 - s][s], self.half(2, dy, 1 - s))

    def y_far(self, dz):
        for s in (0, 1):
            self.l.recv(self.yfar[dz][s], self.half(dz, 2, s))


class RowScatter:
    def __init__(self, links, part, rc, q, xh, xf):
        self.l = links
        self.part, self.rc, self.q, self.xh, self.xf = part, rc, q, xh, xf
        zh, x, c = place()
        self.x, self.c = x, c
        self.xs = [{"dev": dev_of(zh, (x + s) % 4, c)} for s in (1, 3)]
        self.mate = {"dev": dev_of(zh, x, 1 - c)}
        self.dx = (2, 1, 3, 0)

    def block(self, k, other=False):
        return ((self.x + self.dx[k]) % 4) * 2 + (1 - self.c if other else self.c)

    def cores(self):
        self.ch = [self.l.send(self.part.at[self.block(k, True)], self.rc.at[k], self.mate) for k in range(4)]

    def pair_sum(self, k):
        self.l.recv(self.ch[k], self.rc.at[k])
        return self.part[self.block(k)].astype(F32) + self.rc[k].astype(F32)

    def first(self):
        self.q[0] = self.pair_sum(0).astype(BF)
        pieces = halves(self.q, 0)
        self.x1 = [self.l.send(pieces[s], self.xh.at[s], self.xs[s]) for s in (0, 1)]

    def second(self):
        self.x2 = []
        for s in (0, 1):
            value = self.pair_sum(1 + s)
            self.l.recv(self.x1[s], self.xh.at[s])
            arrived = self.xh[s].astype(F32)
            top = value[:16] + arrived if s == 0 else value[:16]
            low = value[16:] + arrived if s == 1 else value[16:]
            self.q[1 + s, pl.ds(0, 16)] = top.astype(BF)
            self.q[1 + s, pl.ds(16, 16)] = low.astype(BF)
            self.x2.append(self.l.send(self.q.at[1 + s], self.xf.at[s], self.xs[s]))

    def total(self):
        value = self.pair_sum(3)
        for s in (0, 1):
            self.l.recv(self.x2[s], self.xf.at[s])
            value = value + self.xf[s].astype(F32)
        return value


class RowGather:
    def __init__(self, links, own, out):
        self.l, self.own, self.out = links, own, out
        zh, x, c = place()
        r = lax.axis_index("req")
        self.x, self.c = x, c
        self.zm = {"req": (1 - r // 4) * 4 + r % 4}
        self.xs = [{"dev": dev_of(zh, (x + s) % 4, c)} for s in (1, 3)]
        self.mate = {"dev": dev_of(zh, x, 1 - c)}
        self.waits, self.xh, self.xfar = [[], []], {}, {}

    def id(self, dx, other=False):
        return ((self.x + dx) % 4) * 2 + (1 - self.c if other else self.c)

    def core(self, row, dx, src=None):
        here, there = self.out.at[row, self.id(dx)], self.out.at[row, self.id(dx, True)]
        self.waits[row].append((self.l.send(here if src is None else src, here, self.mate), there))

    def both_x(self, row, src):
        dst = self.out.at[row, self.id(0)]
        self.xh[row] = [self.l.send(src, dst, to) for to in self.xs]

    def start(self):
        self.zh = self.l.send(self.own, self.out.at[1, self.id(0)], self.zm)
        self.both_x(0, self.own)
        self.core(0, 0, self.own)

    def second(self):
        block = self.out.at[1, self.id(0)]
        self.l.recv(self.zh, block)
        self.both_x(1, block)
        self.core(1, 0)

    def half(self, row, dx, s):
        return self.out.at[row, self.id(dx), pl.ds(16 * s, 16)]

    def near(self, row):
        self.xfar[row] = []
        for s, dx in ((0, 3), (1, 1)):
            self.l.recv(self.xh[row][s], self.out.at[row, self.id(dx)])
            piece = self.half(row, dx, s)
            self.xfar[row].append(self.l.send(piece, piece, self.xs[s]))
            self.core(row, dx)

    def far(self, row):
        for s in (0, 1):
            self.l.recv(self.xfar[row][s], self.half(row, 2, s))
        self.core(row, 2)

    def ready(self, row):
        for handle, region in self.waits[row]:
            self.l.recv(handle, region)


def layer_kernel(
    hid, pool, wq, wkv, wo, gate, up, down, gain_one, gain_two, cosine, sine, bias,
    out, kv_out,
    hid_all, pz, kv_all, wcat, wo_all, wall, nrm, q_all, fresh, s_ref, att_out, att_in,
    part1, rc1, q1, xh1, xf1, residual, n2, rows, act, part2, rc2, q2, xh2, xf2, zsend, zrecv,
    send_sems, recv_sems, local_sems,
):
    zh, x, c = place()
    d = lax.axis_index("dev")
    r = lax.axis_index("req")
    y = r % 4
    width = hid.shape[1]
    links, local = Links(send_sems, recv_sems), Locals(local_sems)
    ag = Gather(links, hid, hid_all)
    ffw = WeightGather(links, (gate, up, down), wall)
    ag2 = RowGather(links, n2, rows)
    mx = x + 1 - 2 * (x % 2)
    mate_x, cross = {"dev": dev_of(zh, mx, c)}, {"dev": dev_of(zh, 3 - x, c)}
    zfar = {"dev": dev_of((zh + 2) % 4, x, c)}
    peers = {m: {"dev": (d + 4 * m) % 32} for m in range(1, 8)}
    greet(ag.zs + ag.xs + [ag.mate, zfar, ag2.zm] + ffw.ys + [peers[m] for m in (1, 3, 5, 7)])

    ag.start()
    ffw.start_y()
    j = (x % 2) * 2 + c
    w_mate = links.send(wkv, wcat.at[2 + j], mate_x)
    w_core = links.send(wkv, wcat.at[2 + j], ag.mate)
    own_pages = local.copy(pool.at[pl.ds(2 * zh, 2)], pz.at[zh])
    local.copy(hid, hid_all.at[d])
    local.copy(wkv, wcat.at[2 + j])
    local.copy(wq, wcat.at[pl.ds(0, 2)])
    own_wo = local.copy(wo, wo_all.at[zh, pl.ds(64, 64)])
    ffw_own = [local.copy(own, wall.at[a, ffw.id(0, 0)]) for a, own in enumerate((gate, up, down))]
    for k in range(4):
        wo_all[k, pl.ds(0, 64)] = jnp.zeros((64, width), BF)

    ag.z_near()
    zstage = []
    for dz, to in ((2, zfar), (1, ag.zs[0]), (3, ag.zs[1])):
        row = (zh + dz) % 4
        zstage.append((links.send(pool.at[pl.ds(2 * row, 2)], pz.at[zh], to), pz.at[(zh + 4 - dz) % 4]))
    quarter = pl.ds(64 + 16 * y, 16)
    wo_own = wo.at[pl.ds(16 * y, 16)]
    wo_z = [links.send(wo_own, wo_all.at[zh, quarter], to) for to in ag.zs]
    ffw.start_z()
    ag.x_near(0)
    ag.z_far()
    own_pages.wait()
    for handle, region in zstage:
        links.recv(handle, region)
    pair = x // 2
    local.copy(pz.at[:, pair], kv_all.at[x * 2 + c])
    p_cross = links.send(pz.at[:, 1 - pair], kv_all.at[x * 2 + c], cross)
    p_mate = links.send(pz.at[:, pair], kv_all.at[x * 2 + c], mate_x)
    p_core = [(links.send(pz.at[:, pair], kv_all.at[x * 2 + c], ag.mate), x)]
    ag.x_near(3)
    ag.x_near(1)
    ag.x_far(0)
    links.recv(w_mate, wcat.at[2 + (1 - x % 2) * 2 + c])
    got = wcat.at[2 + (1 - x % 2) * 2 + c]
    w_fwd = links.send(got, got, ag.mate)
    links.recv(w_core, wcat.at[2 + (x % 2) * 2 + 1 - c])
    ffw.y_own()
    wo_far = []
    for s, dz in ((0, 3), (1, 1)):
        block = (zh + dz) % 4
        links.recv(wo_z[s], wo_all.at[block, quarter])
        piece = wo_all.at[block, quarter, pl.ds(s * (width // 2), width // 2)]
        wo_far.append(links.send(piece, piece, ag.zs[s]))
    links.recv(w_fwd, wcat.at[2 + (1 - x % 2) * 2 + 1 - c])
    for copy in local.copies[1:4]:
        copy.wait()

    lane = lax.broadcasted_iota(jnp.int32, (256, 2 * HD), 1)
    first_half = lane % HD < HD // 2

    def project(dz):
        row = (zh + dz) % 4
        at = pl.ds(pl.multiple_of(row * 256, 256), 256)

        def norm(i, carry):
            nrm[pl.ds(pl.multiple_of(i * 32, 32), 32), :] = root_norm(hid_all[row * 8 + i], gain_one[...])
            return carry

        lax.fori_loop(0, 8, norm, 0)
        projected = transposed_product(nrm[...], wcat[...].reshape(192, width))
        pairs = projected[:, : 2 * HD]
        pairs = jnp.where(lane < HD, pairs, pairs.astype(BF).astype(F32))
        swapped = jnp.where(first_half, pltpu.roll(pairs, 96, 1), pltpu.roll(pairs, 32, 1))
        turned = pairs * cosine[at, :] + swapped * sine[at, :]
        q_all[at, :] = jnp.where(lane < HD, turned * ATTENTION_SCALE, 0.0).astype(BF)
        fresh[at, :] = jnp.concatenate([turned[:, HD:], projected[:, 2 * HD :]], axis=1).astype(BF)

    ag.ready(0)
    project(0)
    ag.x_near_far()
    ag.x_far(3)
    ag.x_far(1)
    got = kv_all.at[(3 - x) * 2 + c]
    links.recv(p_cross, got)
    p_fwd = links.send(got, got, mate_x)
    p_core.append((links.send(got, got, ag.mate), 3 - x))
    ag.ready(3)
    project(3)
    got = kv_all.at[mx * 2 + c]
    links.recv(p_mate, got)
    p_core.append((links.send(got, got, ag.mate), mx))
    ag.ready(1)
    project(1)
    for s in (0, 1):
        links.recv(wo_far[s], wo_all.at[(zh + 2) % 4, quarter, pl.ds(s * (width // 2), width // 2)])
    own_wo.wait()

    def wo_rows(dy):
        return pl.ds(64 + 16 * ((y + dy) % 4), 16)

    wo_y = []
    for to in ffw.ys:
        wo_y.append([links.send(wo_all.at[(zh + dz) % 4, quarter], wo_all.at[(zh + dz) % 4, quarter], to) for dz in (1, 2, 3)])
    ag.x_far(2)
    ag.ready(2)
    project(2)
    got = kv_all.at[(3 - mx) * 2 + c]
    links.recv(p_fwd, got)
    p_core.append((links.send(got, got, ag.mate), 3 - mx))
    kv_h = []
    for m in range(1, 8):
        src = fresh.at[pl.ds(pl.multiple_of(((d + 4 * m) % 32) * 32, 32), 32)]
        kv_h.append(links.send(src, kv_out.at[d // 4], peers[m]))
    own_kv = local.copy(fresh.at[pl.ds(pl.multiple_of(d * 32, 32), 32)], kv_out.at[d // 4])
    for handle, xx in p_core:
        links.recv(handle, kv_all.at[xx * 2 + 1 - c])
    local.copies[4 + 4].wait()

    prefix = 4096
    per_block = KC // 512

    def lanes_max(running, scores):
        for k in range(scores.shape[1] // 128):
            running = jnp.maximum(running, scores[:, k * 128 : (k + 1) * 128])
        return running

    def attend(tile, out_to):
        q = q_all[pl.ds(pl.multiple_of(tile * QT, QT), QT), :]

        def keys_at(i):
            return kv_all[pl.ds(i * per_block, per_block)].reshape(KC, 2 * HD)

        def score_prefix(i, running):
            at = pl.ds(pl.multiple_of(i * KC, KC), KC)
            scores = transposed_product(q, keys_at(i)) + bias[:, at]
            s_ref[:, at] = scores
            return lanes_max(running, scores)

        running = lax.fori_loop(0, prefix // KC, score_prefix, jnp.full((QT, 128), MASKED, F32), unroll=2)
        row = lax.broadcasted_iota(jnp.int32, (QT, QT), 0)
        col = lax.broadcasted_iota(jnp.int32, (QT, QT), 1)

        def score_fresh(i, running):
            at = pl.ds(pl.multiple_of(i * QT, QT), QT)
            scores = transposed_product(q, fresh[at, :])
            scores = jnp.where(col + i * QT <= row + tile * QT, scores, MASKED)
            s_ref[:, pl.ds(pl.multiple_of(prefix + i * QT, QT), QT)] = scores
            return lanes_max(running, scores)

        running = lax.fori_loop(0, tile + 1, score_fresh, running)
        top = jnp.broadcast_to(jnp.max(running, axis=1, keepdims=True), (QT, 128))

        def weigh(at, keys, carried):
            total, summed = carried
            scores = s_ref[:, at]
            pieces = []
            for k in range(scores.shape[1] // 128):
                weights = jnp.exp(scores[:, k * 128 : (k + 1) * 128] - top)
                total = total + weights
                pieces.append(weights.astype(BF))
            weights = jnp.concatenate(pieces, axis=1)
            return total, summed + jnp.dot(weights, keys, preferred_element_type=F32)

        def weigh_prefix(i, carried):
            return weigh(pl.ds(pl.multiple_of(i * KC, KC), KC), keys_at(i), carried)

        def weigh_fresh(i, carried):
            at = pl.ds(pl.multiple_of(prefix + i * QT, QT), QT)
            return weigh(at, fresh[pl.ds(pl.multiple_of(i * QT, QT), QT), :], carried)

        carried = (jnp.zeros((QT, 128), F32), jnp.zeros((QT, 2 * HD), F32))
        carried = lax.fori_loop(0, prefix // KC, weigh_prefix, carried, unroll=2)
        total, summed = lax.fori_loop(0, tile + 1, weigh_fresh, carried)
        out_to[...] = (summed / jnp.sum(total, axis=1, keepdims=True)).astype(BF)

    a2a = []
    steps = weight_steps(ffw)
    for i, (dz, to) in enumerate(((2, zfar), (1, ag.zs[0]), (3, ag.zs[1]))):
        attend((zh + dz) % 4, att_out.at[i])
        a2a.append((links.send(att_out.at[i], att_in.at[zh], to), att_in.at[(zh + 4 - dz) % 4]))
        for step in steps[i]:
            step()
    wo_yfar = []
    for s, dy in ((0, 3), (1, 1)):
        for k, dz in enumerate((1, 2, 3)):
            links.recv(wo_y[s][k], wo_all.at[(zh + dz) % 4, wo_rows(dy)])
        for dz in (1, 2, 3):
            piece = wo_all.at[(zh + dz) % 4, wo_rows(dy), pl.ds(s * (width // 2), width // 2)]
            wo_yfar.append((links.send(piece, piece, ffw.ys[s]), dz, s))
    attend(zh, att_in.at[zh])
    for step in steps[3]:
        step()
    for handle, dz, s in wo_yfar:
        links.recv(handle, wo_all.at[(zh + dz) % 4, wo_rows(2), pl.ds(s * (width // 2), width // 2)])
    for handle, region in a2a:
        links.recv(handle, region)

    one = RowScatter(links, part1, rc1, q1, xh1, xf1)

    def out_columns(n, carry):
        at = pl.ds(pl.multiple_of(n * 512, 512), 512)
        term = None
        for k in (0, 2):
            heads = jnp.concatenate([att_in[k], att_in[k + 1]], axis=1)
            product = jnp.dot(heads, wo_all[pl.ds(k, 2), :, at].reshape(256, 512), preferred_element_type=F32)
            term = product if term is None else term + product
        part1[:, :, at] = term.astype(BF).reshape(8, 32, 512)
        return carry

    lax.fori_loop(0, width // 512, out_columns, 0)
    one.cores()
    one.first()
    one.second()
    residual[...] = one.total() + hid[...].astype(F32)
    n2[...] = root_norm(residual[...], gain_two[...])
    ag2.start()
    own_rows = local.copy(n2, rows.at[0, x * 2 + c])
    for step in steps[4]:
        step()
    ag2.second()
    ag2.near(0)
    ag2.near(1)
    ag2.far(0)
    ag2.far(1)
    ag2.ready(0)
    own_rows.wait()
    for step in steps[5]:
        step()
    for copy in ffw_own:
        copy.wait()

    twos = [RowScatter(links, part2.at[i], rc2.at[i], q2.at[i], xh2.at[i], xf2.at[i]) for i in (0, 1)]

    def feed(row):
        def units(h, carry):
            tokens = rows[row].reshape(256, width)
            some = pl.ds(h * 8, 8)
            gated = transposed_product(tokens, wall[0, some].reshape(256, width))
            raised = transposed_product(tokens, wall[1, some].reshape(256, width))
            act[h] = (gated / (1.0 + jnp.exp(-gated)) * raised).astype(BF)
            return carry

        lax.fori_loop(0, 2, units, 0)

        def columns(n, carry):
            at = pl.ds(pl.multiple_of(n * 512, 512), 512)
            activated = jnp.concatenate([act[0], act[1]], axis=1)
            term = jnp.dot(activated, wall[2, :, :, at].reshape(512, 512), preferred_element_type=F32)
            part2[row, :, :, at] = term.astype(BF).reshape(8, 32, 512)
            return carry

        lax.fori_loop(0, width // 512, columns, 0)

    feed(0)
    twos[0].cores()
    ag2.ready(1)
    feed(1)
    twos[1].cores()
    twos[1].first()
    twos[0].first()
    twos[1].second()
    twos[0].second()
    zsend[...] = twos[1].total().astype(BF)
    last = links.send(zsend, zrecv, ag2.zm)
    value = residual[...] + twos[0].total()
    links.recv(last, zrecv)
    out[...] = (value + zrecv[...].astype(F32)).astype(BF)
    for m in range(1, 8):
        links.recv(kv_h[m - 1], kv_out.at[((d + 32 - 4 * m) % 32) // 4])
    own_kv.wait()
    links.drain()


def weight_steps(ffw):
    return [
        [],
        [ffw.z_near],
        [],
        [ffw.z_far, lambda: ffw.y_near(3), lambda: ffw.y_near(1)],
        [],
        [ffw.y_near_far, lambda: ffw.y_far(0), lambda: ffw.y_far(3), lambda: ffw.y_far(1), lambda: ffw.y_far(2)],
    ]


def vmem(count):
    return [pl.BlockSpec(memory_space=pltpu.VMEM)] * count


def on_device(
    hidden_in, attention_gain, query_weight, keyval_weight, out_weight, feedforward_gain,
    gate_weight, up_weight, down_weight, prefix_pool, page_table, prefix_length,
):
    width = hidden_in.shape[2]
    tokens = 1024
    length = prefix_length[0]
    slots = prefix_pool.shape[1] * PAGE
    pool = prefix_pool[0].transpose(2, 0, 1, 3).reshape(KVH, slots, 2 * HD)

    logical = jnp.sum(
        jnp.where(
            page_table[0][None, :] == jnp.arange(256, dtype=jnp.int32)[:, None],
            jnp.arange(256, dtype=jnp.int32)[None, :],
            0,
        ),
        axis=1,
    )
    slot = logical[:, None] * PAGE + jnp.arange(PAGE, dtype=jnp.int32)[None, :]
    bias = jnp.where(slot < length, 0.0, MASKED).astype(F32)
    bias = bias.reshape(4, 8, slots).transpose(1, 0, 2).reshape(1, 32 * slots)

    positions = (length + jnp.arange(tokens, dtype=jnp.int32)).astype(F32)
    half = HD // 2
    frequency = ROPE_BASE ** (-jnp.arange(half, dtype=F32) / half)
    angles = positions[:, None] * frequency[None, :]
    cosine, sine = jnp.cos(angles), jnp.sin(angles)
    cosine = jnp.concatenate([cosine] * 4, axis=1)
    sine = jnp.concatenate([-sine, sine, -sine, sine], axis=1)

    buffers = [
        ((32, 32, width), BF),
        ((4, 2, slots, 2 * HD), BF),
        ((8, 4, slots, 2 * HD), BF),
        ((6, 32, width), BF),
        ((4, 128, width), BF),
        ((3, 16, 32, width), BF),
        ((256, width), BF),
        ((tokens, 2 * HD), BF),
        ((tokens, 2 * HD), BF),
        ((QT, 32 * slots + tokens), F32),
        ((3, 256, 2 * HD), BF),
        ((4, 256, 2 * HD), BF),
        ((8, 32, width), BF),
        ((4, 32, width), BF),
        ((3, 32, width), BF),
        ((2, 16, width), BF),
        ((2, 32, width), BF),
        ((32, width), F32),
        ((32, width), BF),
        ((2, 8, 32, width), BF),
        ((2, 256, 256), BF),
        ((2, 8, 32, width), BF),
        ((2, 4, 32, width), BF),
        ((2, 3, 32, width), BF),
        ((2, 2, 16, width), BF),
        ((2, 2, 32, width), BF),
        ((32, width), BF),
        ((32, width), BF),
    ]
    hidden_out, kv_out = pl.pallas_call(
        layer_kernel,
        out_shape=[jax.ShapeDtypeStruct((32, width), BF), jax.ShapeDtypeStruct((8, 32, 2 * HD), BF)],
        in_specs=vmem(13),
        out_specs=vmem(2),
        scratch_shapes=[pltpu.VMEM(*b) for b in buffers] + [
            pltpu.SemaphoreType.DMA((COPIES,)),
            pltpu.SemaphoreType.DMA((COPIES,)),
            pltpu.SemaphoreType.DMA((16,)),
        ],
        compiler_params=pltpu.CompilerParams(collective_id=0, has_side_effects=True, vmem_limit_bytes=60 << 20),
        name="layer",
    )(
        hidden_in[0], pool, query_weight.reshape(2, 32, width), keyval_weight, out_weight,
        gate_weight, up_weight, down_weight,
        attention_gain.reshape(1, width), feedforward_gain.reshape(1, width), cosine, sine, bias,
    )
    return hidden_out[None], kv_out.transpose(1, 0, 2)[None]


COPIES = 200


def solution(mesh):
    placed = (
        P("req", "dev", None),
        P(),
        P("dev", None),
        P("dev", None),
        P("dev", None),
        P(),
        P(("req", "dev"), None),
        P(("req", "dev"), None),
        P(("req", "dev"), None),
        P("req", "dev", None, None, None),
        P("req", None),
        P("req"),
    )
    return jax.shard_map(
        on_device,
        mesh=mesh,
        in_specs=placed,
        out_specs=(P("req", "dev", None), P("req", "dev", None, None)),
        check_vma=False,
    )
```

time: 544 us -> 149 us (0.27)
  waiting for transfers between devices: 464 us -> 0 us
  Pallas kernels: 0 us -> 138 us
  matrix products: 29.7 us -> 0 us
  between operations: 16.5 us -> 1.36 us
  other arithmetic: 16.4 us -> 4.5 us
  starting transfers between devices: 7.14 us -> 0 us
    all_gather x6 -> x0, waiting for transfers between devices: 254 us -> none  [the longest x1 65.8 us: on_device(): all_tokens = lax.all_gather(own_tokens, 'dev', axis=0, tiled=True)]
    reduce_scatter x2 -> x0, waiting for transfers between devices: 208 us -> none  [the longest x1 109 us: on_device(): lax.psum_scatter(jnp.dot(rows_in, out_weight, preferred_element_type=jnp....]
    pallas_call x0 -> x1, Pallas kernels: none -> 138 us  [on_device(): pl.pallas_call(layer_kernel, out_shape=[jax.ShapeDtypeStruct((32, width),...]
    dot_general x14 -> x0, matrix products: 29.7 us -> none  [the longest x8 12.1 us: transposed_product(): lax.dot_general(left, right, (((1,), (1,)), ((), ())), preferred_element_...]
    all_to_all x1 -> x0, starting transfers between devices: 6.63 us -> none  [on_device(): lax.all_to_all(outgoing, 'dev', split_axis=2, concat_axis=0, tiled=True)]
    reduce_sum x7 -> x1, other arithmetic: 6.68 us -> 0.11 us  [on_device(): jnp.sum(jnp.where(page_table[0][None, :] == jnp.arange(256, dtype=jnp.int...]
  transfers between devices with their start and end apart: 9 -> 0, of which waited for: 7 -> 0; matrix products, arithmetic and copies ran while one was open for 3% -> 0% of each run, Pallas kernels for 0% -> 0%
where the time goes in v2:
time: 149 us; the launch traced here: 148 us
  Pallas kernels  138 us (93%)
  other arithmetic  4.5 us (3%)
  local copies, waits for them, and re-layouts  3.31 us (2%)
    pallas_call x1, Pallas kernels, on_device(): pl.pallas_call(layer_kernel, out_shape=[jax.ShapeDtypeStruct((32, width),...  138 us

profile of v2, /device:TPU:8, one launch (start us, length us, event | category | flops | bytes accessed | tf_op | source)
XLA Modules:
  0.0 147.6 jit_solution(6559598165214521370)
XLA Ops:
  1.3 1.9 %fusion = (f32[1024,32]{1,0:T(8,128)S(1)}, f32[1024,32]{1,0:T(8,128)S(1)}, f32[1024,32]{1,0:T(8,128)S(1)}) fusion(f32[32]{0:T(128)S(1)} %multiply_power_fusion, f32[1024]{0:T(1024)S(1)} %add_convert_fusion), kind=kLoop, calls=%fused_computation.6 | loop fusion | flops 65536 | bytes 397440 | tf_op jit(solution)/shard_map/neg | solution.py:682
  3.2 0.0 copy-start.2
  3.2 1.8 %pad_maximum_fusion = (f32[1024,128]{1,0:T(8,128)}, f32[1024,128]{1,0:T(8,128)}) fusion(f32[1024,32]{1,0:T(8,128)S(1)} %get-tuple-element.16, f32[1024,32]{1,0:T(8,128)S(1)} %get-tuple-element.15, f32[1024,32]{1,0:T(8,128)S(1)} %get-tuple-element.14), kind=kLoop, calls=%fused_computation.2 | loop fusion | flops 786432 | bytes 1441792 | tf_op jit(solution)/shard_map/concatenate | solution.py:681
  5.1 0.0 copy-start
  5.1 0.0 copy-done.2
  5.1 0.1 select_reduce_fusion
  5.2 0.1 mul.32
  5.3 0.1 add.32
  5.4 0.1 add.33
  5.5 0.1 add.35
  5.6 0.6 fusion.1
  6.2 0.0 copy-done
  6.2 0.7 copy.22
  7.0 138.4 %layer.1 = (bf16[32,2048]{1,0:T(8,128)(2,1)}, bf16[8,32,128]{2,1,0:T(8,128)(2,1)}) custom-call(bf16[32,2048]{1,0:T(8,128)(2,1)} %bitcast.26, bf16[8,128,128]{2,1,0:T(8,128)(2,1)} %bitcast.23, bf16[2,32,2048]{2,1,0:T(8,128)(2,1)} %bitcast.24, bf16[32,2048]{1,0:T(8,128)(2,1)} %wkv.1, bf16[64,2048]{1,0:T(8,128)(2,1)} %wo.1, bf16[32,2048]{1,0:T(8,128)(2,1)} %gate.1, ...), custom_call_target="tpu_custom_call" | custom-call | tf_op jit(solution)/shard_map/layer/pallas_call | solution.py:714
  145.4 0.0 copy-start.1
  145.4 1.5 %copy.25 = bf16[1,32,8,128]{3,2,1,0:T(8,128)(2,1)} copy(bf16[1,32,8,128]{3,1,2,0:T(8,128)(2,1)} %bitcast.29) | data formatting | bytes 131072
  146.9 0.0 copy-done.1
  146.9 0.7 copy.28
  (5 shorter events, 0.0 us)
Async XLA Ops:
  3.2 1.9 %copy-start.2 = (s32[1,256]{1,0:T(1,128)S(1)}, s32[1,256]{1,0:T(1,128)}, u32[]{:S(2)}) copy-start(s32[1,256]{1,0:T(1,128)} %param.22) | copy-start | bytes 3076
  5.1 1.2 copy-start
  145.4 1.5 %copy-start.1 = (bf16[32,2048]{1,0:T(8,128)(2,1)S(1)}, bf16[32,2048]{1,0:T(8,128)(2,1)}, u32[]{:S(2)}) copy-start(bf16[32,2048]{1,0:T(8,128)(2,1)} %get-tuple-element.4) | copy-start | bytes 393220

commit v3 on v2

v3 whole, which is shorter than its diff:
```python
import jax
import jax.numpy as jnp
from jax import lax
from jax.experimental import pallas as pl
from jax.experimental.pallas import tpu as pltpu
from jax.sharding import PartitionSpec as P

MESH = pl.DeviceIdType.MESH
HQ = 32
KVH = 8
HD = 64
PAGE = 16
ROPE_BASE = 10000000.0
EPS = 1e-05
ATTENTION_SCALE = 0.015625
MASKED = -1e30
BF = jnp.bfloat16
F32 = jnp.float32
QT = 256
KC = 1024


def root_norm(activations, norm_gain):
    widened = activations.astype(F32)
    inverse_rms = lax.rsqrt(jnp.mean(widened * widened, axis=-1, keepdims=True) + EPS)
    return (widened * inverse_rms * norm_gain).astype(BF)


def transposed_product(left, right):
    return lax.dot_general(left, right, (((1,), (1,)), ((), ())), preferred_element_type=F32)


def dev_of(zh, x, c):
    return (zh * 4 + x) * 2 + c


def place():
    d = lax.axis_index("dev")
    return d // 8, (d // 2) % 4, d % 2


class Links:
    def __init__(self, send_sems, recv_sems):
        self.send_sems, self.recv_sems = send_sems, recv_sems
        self.copies = []

    def make(self, i, src, dst, to):
        return pltpu.make_async_remote_copy(
            src_ref=src,
            dst_ref=dst,
            send_sem=self.send_sems.at[i],
            recv_sem=self.recv_sems.at[i],
            device_id=to,
            device_id_type=MESH,
        )

    def send(self, src, dst, to):
        i = len(self.copies)
        copy = self.make(i, src, dst, to)
        copy.start()
        self.copies.append(copy)
        return i, to

    def recv(self, handle, region):
        i, to = handle
        self.make(i, region, region, to).wait_recv()

    def drain(self):
        for copy in self.copies:
            copy.wait_send()


class Locals:
    def __init__(self, sems):
        self.sems, self.copies = sems, []

    def copy(self, src, dst):
        copy = pltpu.make_async_copy(src, dst, self.sems.at[len(self.copies)])
        copy.start()
        self.copies.append(copy)
        return copy


def greet(partners):
    barrier = pltpu.get_barrier_semaphore()
    for partner in partners:
        pl.semaphore_signal(barrier, inc=1, device_id=partner, device_id_type=MESH)
    pl.semaphore_wait(barrier, len(partners))


def halves(ref, i):
    rows = ref.shape[1] // 2
    return [ref.at[i, pl.ds(0, rows)], ref.at[i, pl.ds(rows, rows)]]


class Ring:
    def __init__(self, links, i, tos, blk, half, own=None, mate=None, there=None):
        self.l, self.i, self.tos, self.blk, self.half = links, i, tos, blk, half
        self.own = blk(i) if own is None else own
        self.mate, self.there = mate, there
        self.waits = []

    def core(self, j, src=None):
        if self.mate is not None:
            here = self.blk(j)
            self.waits.append((self.l.send(here if src is None else src, here, self.mate), self.there(j)))

    def start(self, core=True):
        mine = self.blk(self.i)
        self.h = [self.l.send(self.own, mine, to) for to in self.tos]
        if core:
            self.core(self.i, self.own)

    def near(self):
        self.f = []
        for s, off in ((0, 3), (1, 1)):
            j = (self.i + off) % 4
            self.l.recv(self.h[s], self.blk(j))
            piece = self.half(j, s)
            self.f.append(self.l.send(piece, piece, self.tos[s]))
            self.core(j)

    def far(self):
        j = (self.i + 2) % 4
        for s in (0, 1):
            self.l.recv(self.f[s], self.half(j, s))
        self.core(j)

    def ready(self):
        for handle, region in self.waits:
            self.l.recv(handle, region)


class PlaneGather:
    def __init__(self, links, own, out):
        self.l, self.own, self.out = links, own, out
        zh, x, c = place()
        r = lax.axis_index("req")
        self.zh, self.zl, self.y = zh, r // 4, r % 4
        self.zs = [{"dev": dev_of((zh + s) % 4, x, c)} for s in (1, 3)]
        self.ys = [{"req": self.zl * 4 + (self.y + s) % 4} for s in (1, 3)]
        self.yh, self.yfar = {}, {}

    def id(self, dz, dy):
        return ((self.zh + dz) % 4) * 4 + (self.y + dy) % 4

    def blk(self, dz, dy):
        return self.out.at[self.id(dz, dy)]

    def half(self, dz, dy, s):
        return self.out.at[self.id(dz, dy), pl.ds(16 * s, 16)]

    def start_y(self):
        self.yh[0] = [self.l.send(self.own, self.blk(0, 0), to) for to in self.ys]

    def start_z(self):
        self.z = [self.l.send(self.own, self.blk(0, 0), to) for to in self.zs]

    def both_y(self, ref):
        return [self.l.send(ref, ref, to) for to in self.ys]

    def z_near(self):
        self.zfar = []
        for s, dz in ((0, 3), (1, 1)):
            self.l.recv(self.z[s], self.blk(dz, 0))
            piece = self.half(dz, 0, s)
            self.zfar.append(self.l.send(piece, piece, self.zs[s]))
            self.yh[dz] = self.both_y(self.blk(dz, 0))

    def z_far(self):
        self.yh2 = []
        for s in (0, 1):
            piece = self.half(2, 0, s)
            self.l.recv(self.zfar[s], piece)
            self.yh2.append(self.both_y(piece))

    def y_near(self, dz):
        self.yfar[dz] = []
        for s, dy in ((0, 3), (1, 1)):
            self.l.recv(self.yh[dz][s], self.blk(dz, dy))
            piece = self.half(dz, dy, s)
            self.yfar[dz].append(self.l.send(piece, piece, self.ys[s]))

    def y_near_far(self):
        self.yfar[2] = []
        for s, dy in ((0, 3), (1, 1)):
            piece = self.half(2, dy, s)
            self.l.recv(self.yh2[s][s], piece)
            self.yfar[2].append(self.l.send(piece, piece, self.ys[s]))
        for s, dy in ((0, 3), (1, 1)):
            self.l.recv(self.yh2[1 - s][s], self.half(2, dy, 1 - s))

    def y_far(self, dz):
        for s in (0, 1):
            self.l.recv(self.yfar[dz][s], self.half(dz, 2, s))


class RowScatter:
    def __init__(self, links, part, rc, q, xh, xf, along_z=False):
        self.l = links
        self.part, self.rc, self.q, self.xh, self.xf = part, rc, q, xh, xf
        zh, x, c = place()
        self.x, self.c = zh if along_z else x, c
        if along_z:
            self.xs = [{"dev": dev_of((zh + s) % 4, x, c)} for s in (1, 3)]
        else:
            self.xs = [{"dev": dev_of(zh, (x + s) % 4, c)} for s in (1, 3)]
        self.mate = {"dev": dev_of(zh, x, 1 - c)}
        self.dx = (2, 1, 3, 0)

    def block(self, k, other=False):
        return ((self.x + self.dx[k]) % 4) * 2 + (1 - self.c if other else self.c)

    def cores(self):
        self.ch = [self.l.send(self.part.at[self.block(k, True)], self.rc.at[k], self.mate) for k in range(4)]

    def pair_sum(self, k):
        self.l.recv(self.ch[k], self.rc.at[k])
        return self.part[self.block(k)].astype(F32) + self.rc[k].astype(F32)

    def first(self):
        self.q[0] = self.pair_sum(0).astype(BF)
        pieces = halves(self.q, 0)
        self.x1 = [self.l.send(pieces[s], self.xh.at[s], self.xs[s]) for s in (0, 1)]

    def second(self):
        self.x2 = []
        for s in (0, 1):
            value = self.pair_sum(1 + s)
            self.l.recv(self.x1[s], self.xh.at[s])
            arrived = self.xh[s].astype(F32)
            top = value[:16] + arrived if s == 0 else value[:16]
            low = value[16:] + arrived if s == 1 else value[16:]
            self.q[1 + s, pl.ds(0, 16)] = top.astype(BF)
            self.q[1 + s, pl.ds(16, 16)] = low.astype(BF)
            self.x2.append(self.l.send(self.q.at[1 + s], self.xf.at[s], self.xs[s]))

    def total(self):
        value = self.pair_sum(3)
        for s in (0, 1):
            self.l.recv(self.x2[s], self.xf.at[s])
            value = value + self.xf[s].astype(F32)
        return value


class RowGather:
    def __init__(self, links, own, out):
        self.l, self.own, self.out = links, own, out
        zh, x, c = place()
        r = lax.axis_index("req")
        self.x, self.c = x, c
        self.zm = {"req": (1 - r // 4) * 4 + r % 4}
        self.xs = [{"dev": dev_of(zh, (x + s) % 4, c)} for s in (1, 3)]
        self.mate = {"dev": dev_of(zh, x, 1 - c)}
        self.waits, self.xh, self.xfar = [[], []], {}, {}

    def id(self, dx, other=False):
        return ((self.x + dx) % 4) * 2 + (1 - self.c if other else self.c)

    def core(self, row, dx, src=None):
        here, there = self.out.at[row, self.id(dx)], self.out.at[row, self.id(dx, True)]
        self.waits[row].append((self.l.send(here if src is None else src, here, self.mate), there))

    def both_x(self, row, src):
        dst = self.out.at[row, self.id(0)]
        self.xh[row] = [self.l.send(src, dst, to) for to in self.xs]

    def start(self):
        self.zh = self.l.send(self.own, self.out.at[1, self.id(0)], self.zm)
        self.both_x(0, self.own)
        self.core(0, 0, self.own)

    def second(self):
        block = self.out.at[1, self.id(0)]
        self.l.recv(self.zh, block)
        self.both_x(1, block)
        self.core(1, 0)

    def half(self, row, dx, s):
        return self.out.at[row, self.id(dx), pl.ds(16 * s, 16)]

    def near(self, row):
        self.xfar[row] = []
        for s, dx in ((0, 3), (1, 1)):
            self.l.recv(self.xh[row][s], self.out.at[row, self.id(dx)])
            piece = self.half(row, dx, s)
            self.xfar[row].append(self.l.send(piece, piece, self.xs[s]))
            self.core(row, dx)

    def far(self, row):
        for s in (0, 1):
            self.l.recv(self.xfar[row][s], self.half(row, 2, s))
        self.core(row, 2)

    def ready(self, row):
        for handle, region in self.waits[row]:
            self.l.recv(handle, region)


def layer_kernel(
    hid, pool, wq, wkv, wo, gate, up, down, gain_one, gain_two, cosine, sine, bias,
    out, kv_out,
    hid_col, relay, kv_all, wq_all, wkv_all, wo_all, wall, nrm, q_all, fresh, s_ref, att,
    part1, rc1, q1, xh1, xf1, residual, n2, rows, act, part2, rc2, q2, xh2, xf2, zsend, zrecv,
    send_sems, recv_sems, local_sems,
):
    zh, x, c = place()
    r = lax.axis_index("req")
    width = hid.shape[1]
    links, local = Links(send_sems, recv_sems), Locals(local_sems)
    zs = [{"dev": dev_of((zh + s) % 4, x, c)} for s in (1, 3)]
    xs = [{"dev": dev_of(zh, (x + s) % 4, c)} for s in (1, 3)]
    mate = {"dev": dev_of(zh, x, 1 - c)}
    planes = [PlaneGather(links, own, wall.at[a]) for a, own in enumerate((gate, up, down))]
    ag2 = RowGather(links, n2, rows)
    column = {(dz, dc): {"dev": dev_of((zh + dz) % 4, x, (c + dc) % 2)} for dz in range(4) for dc in range(2)}
    del column[0, 0]

    hidden = Ring(
        links, zh, zs, lambda j: hid_col.at[j * 2 + c], lambda j, s: hid_col.at[j * 2 + c, pl.ds(16 * s, 16)],
        hid, mate, lambda j: hid_col.at[j * 2 + 1 - c],
    )
    q_ring = Ring(links, x, xs, lambda j: wq_all.at[j], lambda j, s: wq_all.at[j, s], wq)
    kv_ring = Ring(
        links, x, xs, lambda j: wkv_all.at[j * 2 + c], lambda j, s: wkv_all.at[j * 2 + c, pl.ds(16 * s, 16)],
        wkv, mate, lambda j: wkv_all.at[j * 2 + 1 - c],
    )
    pages = Ring(
        links, x, xs, lambda j: kv_all.at[:, j * 2 + c], lambda j, s: kv_all.at[s, j * 2 + c],
        None, mate, lambda j: kv_all.at[:, j * 2 + 1 - c],
    )
    o_ring = Ring(
        links, x, xs, lambda j: wo_all.at[j, pl.ds(64, 64)], lambda j, s: wo_all.at[j, pl.ds(64 + 32 * s, 32)], wo,
    )
    new = Ring(
        links, x, xs, lambda j: fresh.at[c, :, j], lambda j, s: fresh.at[c, pl.ds(2 * s, 2), j],
        None, mate, lambda j: fresh.at[1 - c, :, j],
    )
    greet(list(column.values()) + xs + [ag2.zm] + planes[0].ys)

    mine = x * 2 + c
    near_pages, relayed = [], []
    for s, dz in ((0, 1), (1, 3)):
        near_pages.append(links.send(pool.at[pl.ds(2 * ((zh + dz) % 4), 2)], kv_all.at[:, mine, zh], zs[s]))
        relayed.append(links.send(pool.at[2 * ((zh + 2) % 4) + s], relay.at[s], zs[s]))
    q_ring.start()
    hidden.start()
    kv_ring.start()
    for plane in planes:
        plane.start_y()
    own_pages = local.copy(pool.at[pl.ds(2 * zh, 2)], kv_all.at[:, mine, zh])
    early = [
        local.copy(hid, hid_col.at[zh * 2 + c]),
        local.copy(wkv, wkv_all.at[mine]),
        local.copy(wq, wq_all.at[x]),
    ]
    own_wo = local.copy(wo, wo_all.at[x, pl.ds(64, 64)])
    own_planes = [local.copy(plane.own, plane.blk(0, 0)) for plane in planes]
    far_pages = []
    for s, dz in ((0, 3), (1, 1)):
        links.recv(relayed[s], relay.at[s])
        far_pages.append(links.send(relay.at[s], kv_all.at[s, mine, (zh + dz) % 4], zs[s]))
    for s, dz in ((0, 3), (1, 1)):
        links.recv(near_pages[s], kv_all.at[:, mine, (zh + dz) % 4])
    q_ring.near()
    own_pages.wait()
    for s in (0, 1):
        links.recv(far_pages[s], kv_all.at[s, mine, (zh + 2) % 4])
    pages.start()
    kv_ring.near()
    hidden.near()
    for plane in planes:
        plane.start_z()
    for plane in planes:
        plane.y_near(0)
    for k in range(4):
        wo_all[k, pl.ds(0, 64)] = jnp.zeros((64, width), BF)
    q_ring.far()
    kv_ring.far()
    hidden.far()
    pages.near()
    o_ring.start()
    for copy in early:
        copy.wait()
    hidden.ready()
    kv_ring.ready()

    def norm(i, carry):
        nrm[pl.ds(pl.multiple_of(i * 32, 32), 32), :] = root_norm(hid_col[i], gain_one[...])
        return carry

    lax.fori_loop(0, 8, norm, 0)
    lane = lax.broadcasted_iota(jnp.int32, (256, 2 * HD), 1)
    first_half = lane % HD < HD // 2

    def rotate(pairs):
        swapped = jnp.where(first_half, pltpu.roll(pairs, 96, 1), pltpu.roll(pairs, 32, 1))
        return pairs * cosine[...] + swapped * sine[...]

    keyvals = transposed_product(nrm[...], wkv_all[...].reshape(256, width)).astype(BF)
    for k in (0, 1):
        pairs = keyvals[:, k * 128 : (k + 1) * 128].astype(F32)
        fresh[k, :, x] = jnp.where(lane < HD, rotate(pairs), pairs).astype(BF).reshape(4, 64, 128)
    new.start(False)
    kv_h = []
    for (dz, dc), to in column.items():
        src = fresh.at[c, (zh + dz) % 4, x, pl.ds(32 * ((c + dc) % 2), 32)]
        kv_h.append((links.send(src, kv_out.at[2 * zh + c], to), kv_out.at[2 * ((zh + 4 - dz) % 4) + (c + dc) % 2]))
    own_kv = local.copy(fresh.at[c, zh, x, pl.ds(32 * c, 32)], kv_out.at[2 * zh + c])
    queries = transposed_product(nrm[...], wq_all[...].reshape(256, width))
    for k in (0, 1):
        turned = rotate(queries[:, k * 128 : (k + 1) * 128]) * ATTENTION_SCALE
        for i in (0, 1):
            head = turned if i == 0 else pltpu.roll(turned, 64, 1)
            q_all[k, :, i] = jnp.where(lane < HD, head, 0.0).astype(BF).reshape(4, 64, 128)
    new.near()
    pages.far()
    new.far()
    new.ready()
    pages.ready()

    prefix = 4096
    per_block = KC // 512

    def lanes_max(running, scores):
        for k in range(scores.shape[1] // 128):
            running = jnp.maximum(running, scores[:, k * 128 : (k + 1) * 128])
        return running

    def attend(k, p):
        q = q_all[k, 2 * p : 2 * p + 2].reshape(QT, 2 * HD)

        def keys_at(i):
            return kv_all[k, pl.ds(i * per_block, per_block)].reshape(KC, 2 * HD)

        def score_prefix(i, running):
            at = pl.ds(pl.multiple_of(i * KC, KC), KC)
            scores = transposed_product(q, keys_at(i)) + bias[:, at]
            s_ref[:, at] = scores
            return lanes_max(running, scores)

        running = lax.fori_loop(0, prefix // KC, score_prefix, jnp.full((QT, 128), MASKED, F32), unroll=2)
        row = lax.broadcasted_iota(jnp.int32, (QT, 256), 0)
        token = (2 * p + row // 128) * 256 + x * 64 + row % 64
        col = lax.broadcasted_iota(jnp.int32, (QT, 256), 1)
        for i in range(2 * p + 2):
            scores = transposed_product(q, fresh[k, i].reshape(256, 2 * HD))
            scores = jnp.where(col + i * 256 <= token, scores, MASKED)
            s_ref[:, prefix + i * 256 : prefix + (i + 1) * 256] = scores
            running = lanes_max(running, scores)
        top = jnp.broadcast_to(jnp.max(running, axis=1, keepdims=True), (QT, 128))

        def weigh(at, keys, carried):
            total, summed = carried
            scores = s_ref[:, at]
            pieces = []
            for n in range(scores.shape[1] // 128):
                weights = jnp.exp(scores[:, n * 128 : (n + 1) * 128] - top)
                total = total + weights
                pieces.append(weights.astype(BF))
            weights = jnp.concatenate(pieces, axis=1)
            return total, summed + jnp.dot(weights, keys, preferred_element_type=F32)

        def weigh_prefix(i, carried):
            return weigh(pl.ds(pl.multiple_of(i * KC, KC), KC), keys_at(i), carried)

        carried = (jnp.zeros((QT, 128), F32), jnp.zeros((QT, 2 * HD), F32))
        carried = lax.fori_loop(0, prefix // KC, weigh_prefix, carried, unroll=2)
        for i in range(2 * p + 2):
            carried = weigh(pl.ds(prefix + i * 256, 256), fresh[k, i].reshape(256, 2 * HD), carried)
        total, summed = carried
        mixed = (summed / jnp.sum(total, axis=1, keepdims=True)).astype(BF).reshape(2, 2, 64, 128)
        for z in (0, 1):
            for i in (0, 1):
                att[2 * k + i, (2 * p + z) * 64 : (2 * p + z + 1) * 64] = mixed[z, i]

    steps = weight_steps(planes)
    for n, (k, p) in enumerate(((0, 0), (1, 0), (0, 1), (1, 1))):
        attend(k, p)
        if n == 0:
            o_ring.near()
        if n == 2:
            o_ring.far()
        for step in steps[n]:
            step()
    own_wo.wait()

    one = RowScatter(links, part1, rc1, q1, xh1, xf1, True)

    def out_columns(n, carry):
        at = pl.ds(pl.multiple_of(n * 512, 512), 512)
        term = None
        for k in (0, 2):
            heads = jnp.concatenate([att[k], att[k + 1]], axis=1)
            product = jnp.dot(heads, wo_all[pl.ds(k, 2), :, at].reshape(256, 512), preferred_element_type=F32)
            term = product if term is None else term + product
        part1[:, :, at] = term.astype(BF).reshape(8, 32, 512)
        return carry

    lax.fori_loop(0, width // 512, out_columns, 0)
    one.cores()
    one.first()
    one.second()
    residual[...] = one.total() + hid[...].astype(F32)
    n2[...] = root_norm(residual[...], gain_two[...])
    ag2.start()
    own_rows = local.copy(n2, rows.at[0, x * 2 + c])
    for step in steps[4]:
        step()
    ag2.second()
    ag2.near(0)
    ag2.near(1)
    ag2.far(0)
    ag2.far(1)
    ag2.ready(0)
    own_rows.wait()
    for step in steps[5]:
        step()
    for copy in own_planes:
        copy.wait()

    twos = [RowScatter(links, part2.at[i], rc2.at[i], q2.at[i], xh2.at[i], xf2.at[i]) for i in (0, 1)]

    def feed(row):
        def units(h, carry):
            tokens = rows[row].reshape(256, width)
            some = pl.ds(h * 8, 8)
            gated = transposed_product(tokens, wall[0, some].reshape(256, width))
            raised = transposed_product(tokens, wall[1, some].reshape(256, width))
            act[h] = (gated / (1.0 + jnp.exp(-gated)) * raised).astype(BF)
            return carry

        lax.fori_loop(0, 2, units, 0)

        def columns(n, carry):
            at = pl.ds(pl.multiple_of(n * 512, 512), 512)
            activated = jnp.concatenate([act[0], act[1]], axis=1)
            term = jnp.dot(activated, wall[2, :, :, at].reshape(512, 512), preferred_element_type=F32)
            part2[row, :, :, at] = term.astype(BF).reshape(8, 32, 512)
            return carry

        lax.fori_loop(0, width // 512, columns, 0)

    feed(0)
    twos[0].cores()
    ag2.ready(1)
    feed(1)
    twos[1].cores()
    twos[1].first()
    twos[0].first()
    twos[1].second()
    twos[0].second()
    zsend[...] = twos[1].total().astype(BF)
    last = links.send(zsend, zrecv, ag2.zm)
    value = residual[...] + twos[0].total()
    links.recv(last, zrecv)
    out[...] = (value + zrecv[...].astype(F32)).astype(BF)
    for handle, region in kv_h:
        links.recv(handle, region)
    own_kv.wait()
    links.drain()


def weight_steps(planes):
    gate, up, down = planes

    def near(plane):
        return [lambda: plane.y_near(3), lambda: plane.y_near(1)]

    def last(plane):
        return [plane.y_near_far] + [lambda dz=dz: plane.y_far(dz) for dz in (0, 3, 1, 2)]

    return [
        [gate.z_near],
        [up.z_near],
        [down.z_near] + near(gate),
        [],
        [gate.z_far] + near(up) + [up.z_far] + near(down) + [down.z_far],
        last(gate) + last(up) + last(down),
    ]


def vmem(count):
    return [pl.BlockSpec(memory_space=pltpu.VMEM)] * count


def on_device(
    hidden_in, attention_gain, query_weight, keyval_weight, out_weight, feedforward_gain,
    gate_weight, up_weight, down_weight, prefix_pool, page_table, prefix_length,
):
    width = hidden_in.shape[2]
    tokens = 1024
    length = prefix_length[0]
    slots = prefix_pool.shape[1] * PAGE
    pool = prefix_pool[0].transpose(2, 0, 1, 3).reshape(KVH, slots, 2 * HD)

    logical = jnp.sum(
        jnp.where(
            page_table[0][None, :] == jnp.arange(256, dtype=jnp.int32)[:, None],
            jnp.arange(256, dtype=jnp.int32)[None, :],
            0,
        ),
        axis=1,
    )
    slot = logical[:, None] * PAGE + jnp.arange(PAGE, dtype=jnp.int32)[None, :]
    bias = jnp.where(slot < length, 0.0, MASKED).astype(F32)
    bias = bias.reshape(4, 8, slots).transpose(1, 0, 2).reshape(1, 32 * slots)

    index = jnp.arange(256, dtype=jnp.int32)
    column = (lax.axis_index("dev") // 2) % 4
    positions = (length + index // 64 * 256 + column * 64 + index % 64).astype(F32)
    half = HD // 2
    frequency = ROPE_BASE ** (-jnp.arange(half, dtype=F32) / half)
    angles = positions[:, None] * frequency[None, :]
    cosine, sine = jnp.cos(angles), jnp.sin(angles)
    cosine = jnp.concatenate([cosine] * 4, axis=1)
    sine = jnp.concatenate([-sine, sine, -sine, sine], axis=1)

    buffers = [
        ((8, 32, width), BF),
        ((2, slots, 2 * HD), BF),
        ((2, 8, 4, slots, 2 * HD), BF),
        ((4, 2, 32, width), BF),
        ((8, 32, width), BF),
        ((4, 128, width), BF),
        ((3, 16, 32, width), BF),
        ((256, width), BF),
        ((2, 4, 2, 64, 2 * HD), BF),
        ((2, 4, 4, 64, 2 * HD), BF),
        ((QT, 32 * slots + tokens), F32),
        ((4, 256, 2 * HD), BF),
        ((8, 32, width), BF),
        ((4, 32, width), BF),
        ((3, 32, width), BF),
        ((2, 16, width), BF),
        ((2, 32, width), BF),
        ((32, width), F32),
        ((32, width), BF),
        ((2, 8, 32, width), BF),
        ((2, 256, 256), BF),
        ((2, 8, 32, width), BF),
        ((2, 4, 32, width), BF),
        ((2, 3, 32, width), BF),
        ((2, 2, 16, width), BF),
        ((2, 2, 32, width), BF),
        ((32, width), BF),
        ((32, width), BF),
    ]
    hidden_out, kv_out = pl.pallas_call(
        layer_kernel,
        out_shape=[jax.ShapeDtypeStruct((32, width), BF), jax.ShapeDtypeStruct((8, 32, 2 * HD), BF)],
        in_specs=vmem(13),
        out_specs=vmem(2),
        scratch_shapes=[pltpu.VMEM(*b) for b in buffers] + [
            pltpu.SemaphoreType.DMA((COPIES,)),
            pltpu.SemaphoreType.DMA((COPIES,)),
            pltpu.SemaphoreType.DMA((16,)),
        ],
        compiler_params=pltpu.CompilerParams(collective_id=0, has_side_effects=True, vmem_limit_bytes=60 << 20),
        name="layer",
    )(
        hidden_in[0], pool, query_weight.reshape(2, 32, width), keyval_weight, out_weight,
        gate_weight, up_weight, down_weight,
        attention_gain.reshape(1, width), feedforward_gain.reshape(1, width), cosine, sine, bias,
    )
    return hidden_out[None], kv_out.transpose(1, 0, 2)[None]


COPIES = 230


def solution(mesh):
    placed = (
        P("req", "dev", None),
        P(),
        P("dev", None),
        P("dev", None),
        P("dev", None),
        P(),
        P(("req", "dev"), None),
        P(("req", "dev"), None),
        P(("req", "dev"), None),
        P("req", "dev", None, None, None),
        P("req", None),
        P("req"),
    )
    return jax.shard_map(
        on_device,
        mesh=mesh,
        in_specs=placed,
        out_specs=(P("req", "dev", None), P("req", "dev", None, None)),
        check_vma=False,
    )
```

time: 149 us -> 135 us (0.906)
  Pallas kernels: 138 us -> 126 us
  other arithmetic: 4.5 us -> 2.26 us
    pallas_call x1, Pallas kernels: 138 us -> 126 us  [on_device(): pl.pallas_call(layer_kernel, out_shape=[jax.ShapeDtypeStruct((32, width),...]
where the time goes in v3:
time: 135 us; the launch traced here: 133 us
  Pallas kernels  126 us (93%)
  local copies, waits for them, and re-layouts  3.3 us (2%)
  other arithmetic  2.26 us (2%)
  between operations  1.39 us (1%)
    pallas_call x1, Pallas kernels, on_device(): pl.pallas_call(layer_kernel, out_shape=[jax.ShapeDtypeStruct((32, width),...  126 us

profile of v3, /device:TPU:8, one launch (start us, length us, event | category | flops | bytes accessed | tf_op | source)
XLA Modules:
  0.0 132.6 jit_solution(14076895104726762871)
XLA Ops:
  1.3 0.5 fusion
  1.9 0.0 copy-start.2
  1.9 1.0 pad_maximum_fusion
  2.9 0.0 copy-start
  2.9 0.0 copy-done.2
  2.9 0.1 select_reduce_fusion
  3.0 0.1 mul.48
  3.1 0.1 add.74
  3.2 0.1 add.75
  3.3 0.1 add.77
  3.4 0.6 fusion.1
  4.0 0.0 copy-done
  4.0 0.7 copy.22
  4.7 125.6 %layer.1 = (bf16[32,2048]{1,0:T(8,128)(2,1)}, bf16[8,32,128]{2,1,0:T(8,128)(2,1)}) custom-call(bf16[32,2048]{1,0:T(8,128)(2,1)} %bitcast.27, bf16[8,128,128]{2,1,0:T(8,128)(2,1)} %bitcast.23, bf16[2,32,2048]{2,1,0:T(8,128)(2,1)} %bitcast.25, bf16[32,2048]{1,0:T(8,128)(2,1)} %wkv.1, bf16[64,2048]{1,0:T(8,128)(2,1)} %wo.1, bf16[32,2048]{1,0:T(8,128)(2,1)} %gate.1, ...), custom_call_target="tpu_custom_call" | custom-call | tf_op jit(solution)/shard_map/layer/pallas_call | solution.py:649
  130.4 0.0 copy-start.1
  130.4 1.5 %copy.25 = bf16[1,32,8,128]{3,2,1,0:T(8,128)(2,1)} copy(bf16[1,32,8,128]{3,1,2,0:T(8,128)(2,1)} %bitcast.29) | data formatting | bytes 131072
  131.9 0.0 copy-done.1
  131.9 0.7 copy.28
  (5 shorter events, 0.0 us)
Async XLA Ops:
  1.9 1.0 copy-start.2
  2.9 1.2 copy-start
  130.4 1.5 %copy-start.1 = (bf16[32,2048]{1,0:T(8,128)(2,1)S(1)}, bf16[32,2048]{1,0:T(8,128)(2,1)}, u32[]{:S(2)}) copy-start(bf16[32,2048]{1,0:T(8,128)(2,1)} %get-tuple-element.4) | copy-start | bytes 393220

commit v4 on v3

--- a/solution.py
+++ b/solution.py
@@ -132,67 +132,74 @@
 
 
 class PlaneGather:
-    def __init__(self, links, own, out):
-        self.l, self.own, self.out = links, own, out
+    def __init__(self, links, out, x_first):
+        self.l, self.out, self.x_first = links, out, x_first
         zh, x, c = place()
         r = lax.axis_index("req")
-        self.zh, self.zl, self.y = zh, r // 4, r % 4
-        self.zs = [{"dev": dev_of((zh + s) % 4, x, c)} for s in (1, 3)]
-        self.ys = [{"req": self.zl * 4 + (self.y + s) % 4} for s in (1, 3)]
-        self.yh, self.yfar = {}, {}
-
-    def id(self, dz, dy):
-        return ((self.zh + dz) % 4) * 4 + (self.y + dy) % 4
-
-    def blk(self, dz, dy):
-        return self.out.at[self.id(dz, dy)]
-
-    def half(self, dz, dy, s):
-        return self.out.at[self.id(dz, dy), pl.ds(16 * s, 16)]
-
-    def start_y(self):
-        self.yh[0] = [self.l.send(self.own, self.blk(0, 0), to) for to in self.ys]
-
-    def start_z(self):
-        self.z = [self.l.send(self.own, self.blk(0, 0), to) for to in self.zs]
-
-    def both_y(self, ref):
-        return [self.l.send(ref, ref, to) for to in self.ys]
-
-    def z_near(self):
-        self.zfar = []
-        for s, dz in ((0, 3), (1, 1)):
-            self.l.recv(self.z[s], self.blk(dz, 0))
-            piece = self.half(dz, 0, s)
-            self.zfar.append(self.l.send(piece, piece, self.zs[s]))
-            self.yh[dz] = self.both_y(self.blk(dz, 0))
-
-    def z_far(self):
-        self.yh2 = []
+        self.x, self.y, self.rows = x, r % 4, pl.ds(0 if x_first else 16, 16)
+        xs = [{"dev": dev_of(zh, (x + s) % 4, c)} for s in (1, 3)]
+        ys = [{"req": r // 4 * 4 + (self.y + s) % 4} for s in (1, 3)]
+        self.one, self.two = (xs, ys) if x_first else (ys, xs)
+        self.h2, self.f2 = {}, {}
+
+    def id(self, a, b):
+        dx, dy = (a, b) if self.x_first else (b, a)
+        return (self.x + dx) % 4 * 4 + (self.y + dy) % 4
+
+    def blk(self, a, b):
+        return self.out.at[:, self.id(a, b), self.rows]
+
+    def half(self, a, b, s):
+        wide = self.out.shape[3] // 2
+        return self.out.at[:, self.id(a, b), self.rows, pl.ds(s * wide, wide)]
+
+    def both(self, ref, tos):
+        return [self.l.send(ref, ref, to) for to in tos]
+
+    def start_one(self):
+        self.h1 = self.both(self.blk(0, 0), self.one)
+
+    def start_two(self):
+        self.h2[0] = self.both(self.blk(0, 0), self.two)
+
+    def near_one(self):
+        self.f1 = []
+        for s, a in ((0, 3), (1, 1)):
+            self.l.recv(self.h1[s], self.blk(a, 0))
+            piece = self.half(a, 0, s)
+            self.f1.append(self.l.send(piece, piece, self.one[s]))
+
+    def spread(self):
+        for a in (3, 1):
+            self.h2[a] = self.both(self.blk(a, 0), self.two)
+
+    def far_one(self):
+        self.g2 = []
         for s in (0, 1):
             piece = self.half(2, 0, s)
-            self.l.recv(self.zfar[s], piece)
-            self.yh2.append(self.both_y(piece))
-
-    def y_near(self, dz):
-        self.yfar[dz] = []
-        for s, dy in ((0, 3), (1, 1)):
-            self.l.recv(self.yh[dz][s], self.blk(dz, dy))
-            piece = self.half(dz, dy, s)
-            self.yfar[dz].append(self.l.send(piece, piece, self.ys[s]))
-
-    def y_near_far(self):
-        self.yfar[2] = []
-        for s, dy in ((0, 3), (1, 1)):
-            piece = self.half(2, dy, s)
-            self.l.recv(self.yh2[s][s], piece)
-            self.yfar[2].append(self.l.send(piece, piece, self.ys[s]))
-        for s, dy in ((0, 3), (1, 1)):
-            self.l.recv(self.yh2[1 - s][s], self.half(2, dy, 1 - s))
-
-    def y_far(self, dz):
-        for s in (0, 1):
-            self.l.recv(self.yfar[dz][s], self.half(dz, 2, s))
+            self.l.recv(self.f1[s], piece)
+            self.g2.append(self.both(piece, self.two))
+
+    def near_two(self, a):
+        self.f2[a] = []
+        for s, b in ((0, 3), (1, 1)):
+            self.l.recv(self.h2[a][s], self.blk(a, b))
+            piece = self.half(a, b, s)
+            self.f2[a].append(self.l.send(piece, piece, self.two[s]))
+
+    def near_two_far(self):
+        self.f2[2] = []
+        for s, b in ((0, 3), (1, 1)):
+            piece = self.half(2, b, s)
+            self.l.recv(self.g2[s][s], piece)
+            self.f2[2].append(self.l.send(piece, piece, self.two[s]))
+        for s, b in ((0, 3), (1, 1)):
+            self.l.recv(self.g2[1 - s][s], self.half(2, b, 1 - s))
+
+    def far_two(self):
+        for a in (0, 3, 1, 2):
+            for s in (0, 1):
+                self.l.recv(self.f2[a][s], self.half(a, 2, s))
 
 
 class RowScatter:
@@ -243,65 +250,109 @@
         return value
 
 
-class RowGather:
-    def __init__(self, links, own, out):
-        self.l, self.own, self.out = links, own, out
+def z_neighbours():
+    zh, x, c = place()
+    r = lax.axis_index("req")
+    z = zh * 2 + r // 4
+    tos = []
+    for step in (1, 7):
+        other = (z + step) % 8
+        tos.append({"req": other % 2 * 4 + r % 4, "dev": dev_of(other // 2, x, c)})
+    return tos
+
+
+class ColumnGather:
+    def __init__(self, links, out):
+        self.l, self.out = links, out
+        self.tos = z_neighbours()
         zh, x, c = place()
-        r = lax.axis_index("req")
-        self.x, self.c = x, c
-        self.zm = {"req": (1 - r // 4) * 4 + r % 4}
-        self.xs = [{"dev": dev_of(zh, (x + s) % 4, c)} for s in (1, 3)]
         self.mate = {"dev": dev_of(zh, x, 1 - c)}
-        self.waits, self.xh, self.xfar = [[], []], {}, {}
-
-    def id(self, dx, other=False):
-        return ((self.x + dx) % 4) * 2 + (1 - self.c if other else self.c)
-
-    def core(self, row, dx, src=None):
-        here, there = self.out.at[row, self.id(dx)], self.out.at[row, self.id(dx, True)]
-        self.waits[row].append((self.l.send(here if src is None else src, here, self.mate), there))
-
-    def both_x(self, row, src):
-        dst = self.out.at[row, self.id(0)]
-        self.xh[row] = [self.l.send(src, dst, to) for to in self.xs]
+        self.h, self.waits = {}, {}
+
+    def piece(self, k, p):
+        return self.out.at[k % 8, 0, pl.ds(16 * p, 16)]
+
+    def core(self, k):
+        self.waits[k % 8] = self.l.send(self.out.at[k % 8, 0], self.out.at[k % 8, 1], self.mate)
+
+    def pass_on(self, s, k, p):
+        sign = -1 if s == 0 else 1
+        self.h[s, k + 1, p] = self.l.send(self.piece(sign * k, p), self.piece(sign * (k + 1), p), self.tos[s])
 
     def start(self):
-        self.zh = self.l.send(self.own, self.out.at[1, self.id(0)], self.zm)
-        self.both_x(0, self.own)
-        self.core(0, 0, self.own)
-
-    def second(self):
-        block = self.out.at[1, self.id(0)]
-        self.l.recv(self.zh, block)
-        self.both_x(1, block)
-        self.core(1, 0)
-
-    def half(self, row, dx, s):
-        return self.out.at[row, self.id(dx), pl.ds(16 * s, 16)]
-
-    def near(self, row):
-        self.xfar[row] = []
-        for s, dx in ((0, 3), (1, 1)):
-            self.l.recv(self.xh[row][s], self.out.at[row, self.id(dx)])
-            piece = self.half(row, dx, s)
-            self.xfar[row].append(self.l.send(piece, piece, self.xs[s]))
-            self.core(row, dx)
-
-    def far(self, row):
+        for p in (0, 1):
+            for s in (0, 1):
+                self.pass_on(s, 0, p if s == 0 else 1 - p)
+        self.core(0)
+
+    def hop(self, k):
+        for p in (0, 1):
+            for s in (0, 1):
+                q = p if s == 0 else 1 - p
+                self.l.recv(self.h[s, k, q], self.piece(-k if s == 0 else k, q))
+                if k < 3 or q == s:
+                    self.pass_on(s, k, q)
+        self.core(k)
+        self.core(-k)
+
+    def last(self):
         for s in (0, 1):
-            self.l.recv(self.xfar[row][s], self.half(row, 2, s))
-        self.core(row, 2)
-
-    def ready(self, row):
-        for handle, region in self.waits[row]:
-            self.l.recv(handle, region)
+            self.l.recv(self.h[s, 4, s], self.piece(4, s))
+        self.core(4)
+
+    def ready(self, ks):
+        for k in ks:
+            self.l.recv(self.waits[k % 8], self.out.at[k % 8, 1])
+
+
+class ColumnScatter:
+    def __init__(self, links, part, rc, q, arrived):
+        self.l, self.part, self.rc, self.q, self.arrived = links, part, rc, q, arrived
+        self.tos = z_neighbours()
+        zh, x, c = place()
+        self.mate = {"dev": dev_of(zh, x, 1 - c)}
+        self.ch, self.h = {}, {}
+
+    def cores(self, ks):
+        for k in ks:
+            self.ch[k] = self.l.send(self.part.at[k, 1], self.rc.at[k], self.mate)
+
+    def arrive(self, ks):
+        for k in ks:
+            self.l.recv(self.ch[k], self.rc.at[k])
+
+    def own(self, k, p):
+        at = pl.ds(16 * p, 16)
+        return self.part[k % 8, 0, at].astype(F32) + self.rc[k % 8, at].astype(F32)
+
+    def hop(self, k):
+        for p in (0, 1):
+            for s in (0, 1):
+                q = p if s == 0 else 1 - p
+                if k == 4 and q != s:
+                    continue
+                value = self.own(k if s == 0 else -k, q)
+                if (s, k + 1, q) in self.h:
+                    slot = self.arrived.at[s, k + 1 - 2, q]
+                    self.l.recv(self.h[s, k + 1, q], slot)
+                    value = value + slot[...].astype(F32)
+                self.q[s, k - 1, q] = value.astype(BF)
+                self.h[s, k, q] = self.l.send(self.q.at[s, k - 1, q], self.arrived.at[s, (k - 2) % 4, q], self.tos[s])
+
+    def total(self, p):
+        value = self.own(0, p)
+        for s in (0, 1):
+            slot = self.arrived.at[s, 3, p]
+            self.l.recv(self.h[s, 1, p], slot)
+            value = value + slot[...].astype(F32)
+        return value
 
 
 def layer_kernel(
     hid, pool, wq, wkv, wo, gate, up, down, gain_one, gain_two, cosine, sine, bias,
     out, kv_out,
     hid_col, relay, kv_all, wq_all, wkv_all, wo_all, wall, nrm, q_all, fresh, s_ref, att,
-    part1, rc1, q1, xh1, xf1, residual, n2, rows, act, part2, rc2, q2, xh2, xf2, zsend, zrecv,
+    part1, rc1, q1, xh1, xf1, residual, rows, act, part2, rc2, q2, arrived2,
     send_sems, recv_sems, local_sems,
 ):
     zh, x, c = place()
@@ -311,8 +362,10 @@
     zs = [{"dev": dev_of((zh + s) % 4, x, c)} for s in (1, 3)]
     xs = [{"dev": dev_of(zh, (x + s) % 4, c)} for s in (1, 3)]
     mate = {"dev": dev_of(zh, x, 1 - c)}
-    planes = [PlaneGather(links, own, wall.at[a]) for a, own in enumerate((gate, up, down))]
-    ag2 = RowGather(links, n2, rows)
+    y = r % 4
+    ys = [{"req": r // 4 * 4 + (y + s) % 4} for s in (1, 3)]
+    a_plane, b_plane = PlaneGather(links, wall, True), PlaneGather(links, wall, False)
+    ag2 = ColumnGather(links, rows)
     column = {(dz, dc): {"dev": dev_of((zh + dz) % 4, x, (c + dc) % 2)} for dz in range(4) for dc in range(2)}
     del column[0, 0]
 
@@ -320,11 +373,32 @@
         links, zh, zs, lambda j: hid_col.at[j * 2 + c], lambda j, s: hid_col.at[j * 2 + c, pl.ds(16 * s, 16)],
         hid, mate, lambda j: hid_col.at[j * 2 + 1 - c],
     )
-    q_ring = Ring(links, x, xs, lambda j: wq_all.at[j], lambda j, s: wq_all.at[j, s], wq)
+    wide = width // 4
+
+    def quarter(k):
+        return pl.ds(pl.multiple_of(k * wide, wide), wide)
+
+    q_ring = Ring(
+        links, x, xs, lambda j: wq_all.at[j, :, :, quarter(y)], lambda j, s: wq_all.at[j, s, :, quarter(y)],
+        wq.at[:, :, quarter(y)],
+    )
     kv_ring = Ring(
-        links, x, xs, lambda j: wkv_all.at[j * 2 + c], lambda j, s: wkv_all.at[j * 2 + c, pl.ds(16 * s, 16)],
-        wkv, mate, lambda j: wkv_all.at[j * 2 + 1 - c],
-    )
+        links, x, xs, lambda j: wkv_all.at[j * 2 + c, :, quarter(y)],
+        lambda j, s: wkv_all.at[j * 2 + c, pl.ds(16 * s, 16), quarter(y)], wkv.at[:, quarter(y)],
+    )
+    y_rings = {}
+    for dx in (1, 2, 3):
+        j = (x + dx) % 4
+        y_rings[dx] = [
+            Ring(
+                links, y, ys, lambda k, j=j: wkv_all.at[j * 2 + c, :, quarter(k)],
+                lambda k, s, j=j: wkv_all.at[j * 2 + c, pl.ds(16 * s, 16), quarter(k)],
+            ),
+            Ring(
+                links, y, ys, lambda k, j=j: wq_all.at[j, :, :, quarter(k)],
+                lambda k, s, j=j: wq_all.at[j, s, :, quarter(k)],
+            ),
+        ]
     pages = Ring(
         links, x, xs, lambda j: kv_all.at[:, j * 2 + c], lambda j, s: kv_all.at[s, j * 2 + c],
         None, mate, lambda j: kv_all.at[:, j * 2 + 1 - c],
@@ -336,18 +410,18 @@
         links, x, xs, lambda j: fresh.at[c, :, j], lambda j, s: fresh.at[c, pl.ds(2 * s, 2), j],
         None, mate, lambda j: fresh.at[1 - c, :, j],
     )
-    greet(list(column.values()) + xs + [ag2.zm] + planes[0].ys)
+    greet(list(column.values()) + xs + ag2.tos + ys)
 
     mine = x * 2 + c
     near_pages, relayed = [], []
     for s, dz in ((0, 1), (1, 3)):
         near_pages.append(links.send(pool.at[pl.ds(2 * ((zh + dz) % 4), 2)], kv_all.at[:, mine, zh], zs[s]))
         relayed.append(links.send(pool.at[2 * ((zh + 2) % 4) + s], relay.at[s], zs[s]))
+    kv_ring.start()
     q_ring.start()
     hidden.start()
-    kv_ring.start()
-    for plane in planes:
-        plane.start_y()
+    w_core = [(links.send(wkv, wkv_all.at[mine], mate), wkv_all.at[x * 2 + 1 - c])]
+    own_planes = [local.copy(own, wall.at[a, x * 4 + y]) for a, own in enumerate((gate, up, down))]
     own_pages = local.copy(pool.at[pl.ds(2 * zh, 2)], kv_all.at[:, mine, zh])
     early = [
         local.copy(hid, hid_col.at[zh * 2 + c]),
@@ -355,35 +429,52 @@
         local.copy(wq, wq_all.at[x]),
     ]
     own_wo = local.copy(wo, wo_all.at[x, pl.ds(64, 64)])
-    own_planes = [local.copy(plane.own, plane.blk(0, 0)) for plane in planes]
+    kv_ring.near()
+    q_ring.near()
+    for dx in (1, 3):
+        for ring in y_rings[dx]:
+            ring.start()
+    for copy in own_planes:
+        copy.wait()
+    a_plane.start_one()
+    kv_ring.far()
+    q_ring.far()
+    for ring in y_rings[2]:
+        ring.start()
+    b_plane.start_one()
+    a_plane.start_two()
     far_pages = []
     for s, dz in ((0, 3), (1, 1)):
         links.recv(relayed[s], relay.at[s])
         far_pages.append(links.send(relay.at[s], kv_all.at[s, mine, (zh + dz) % 4], zs[s]))
+    for dx in (1, 3):
+        for ring in y_rings[dx]:
+            ring.near()
+    a_plane.near_one()
     for s, dz in ((0, 3), (1, 1)):
         links.recv(near_pages[s], kv_all.at[:, mine, (zh + dz) % 4])
-    q_ring.near()
     own_pages.wait()
     for s in (0, 1):
         links.recv(far_pages[s], kv_all.at[s, mine, (zh + 2) % 4])
     pages.start()
-    kv_ring.near()
+    for ring in y_rings[2]:
+        ring.near()
     hidden.near()
-    for plane in planes:
-        plane.start_z()
-    for plane in planes:
-        plane.y_near(0)
     for k in range(4):
         wo_all[k, pl.ds(0, 64)] = jnp.zeros((64, width), BF)
-    q_ring.far()
-    kv_ring.far()
+    for copy in early:
+        copy.wait()
+    for dx in (1, 3, 2):
+        for ring in y_rings[dx]:
+            ring.far()
+        block = (x + dx) % 4 * 2
+        w_core.append((links.send(wkv_all.at[block + c], wkv_all.at[block + c], mate), wkv_all.at[block + 1 - c]))
+    a_plane.spread()
     hidden.far()
     pages.near()
-    o_ring.start()
-    for copy in early:
-        copy.wait()
     hidden.ready()
-    kv_ring.ready()
+    for handle, region in w_core:
+        links.recv(handle, region)
 
     def norm(i, carry):
         nrm[pl.ds(pl.multiple_of(i * 32, 32), 32), :] = root_norm(hid_col[i], gain_one[...])
@@ -414,8 +505,11 @@
             head = turned if i == 0 else pltpu.roll(turned, 64, 1)
             q_all[k, :, i] = jnp.where(lane < HD, head, 0.0).astype(BF).reshape(4, 64, 128)
     new.near()
+    o_ring.start()
     pages.far()
     new.far()
+    a_plane.far_one()
+    b_plane.near_one()
     new.ready()
     pages.ready()
 
@@ -474,15 +568,18 @@
             for i in (0, 1):
                 att[2 * k + i, (2 * p + z) * 64 : (2 * p + z + 1) * 64] = mixed[z, i]
 
-    steps = weight_steps(planes)
-    for n, (k, p) in enumerate(((0, 0), (1, 0), (0, 1), (1, 1))):
-        attend(k, p)
-        if n == 0:
-            o_ring.near()
-        if n == 2:
-            o_ring.far()
-        for step in steps[n]:
-            step()
+    attend(0, 0)
+    o_ring.near()
+    b_plane.start_two()
+    b_plane.spread()
+    a_plane.near_two(0)
+    attend(1, 0)
+    b_plane.far_one()
+    a_plane.near_two(3)
+    attend(0, 1)
+    o_ring.far()
+    a_plane.near_two(1)
+    attend(1, 1)
     own_wo.wait()
 
     one = RowScatter(links, part1, rc1, q1, xh1, xf1, True)
@@ -502,31 +599,30 @@
     one.first()
     one.second()
     residual[...] = one.total() + hid[...].astype(F32)
-    n2[...] = root_norm(residual[...], gain_two[...])
+    rows[0, 0] = root_norm(residual[...], gain_two[...])
     ag2.start()
-    own_rows = local.copy(n2, rows.at[0, x * 2 + c])
-    for step in steps[4]:
-        step()
-    ag2.second()
-    ag2.near(0)
-    ag2.near(1)
-    ag2.far(0)
-    ag2.far(1)
-    ag2.ready(0)
-    own_rows.wait()
-    for step in steps[5]:
-        step()
-    for copy in own_planes:
-        copy.wait()
-
-    twos = [RowScatter(links, part2.at[i], rc2.at[i], q2.at[i], xh2.at[i], xf2.at[i]) for i in (0, 1)]
-
-    def feed(row):
+    a_plane.near_two_far()
+    b_plane.near_two(0)
+    ag2.hop(1)
+    ag2.hop(2)
+    ag2.hop(3)
+    b_plane.near_two(3)
+    b_plane.near_two(1)
+    b_plane.near_two_far()
+    a_plane.far_two()
+    ag2.ready((0, 1, 7, 2))
+    b_plane.far_two()
+
+    two = ColumnScatter(links, part2, rc2, q2, arrived2)
+
+    def feed(ks):
+        tokens = jnp.concatenate([rows[k].reshape(64, width) for k in ks], axis=0)
+        nrm[...] = tokens
+
         def units(h, carry):
-            tokens = rows[row].reshape(256, width)
             some = pl.ds(h * 8, 8)
-            gated = transposed_product(tokens, wall[0, some].reshape(256, width))
-            raised = transposed_product(tokens, wall[1, some].reshape(256, width))
+            gated = transposed_product(nrm[...], wall[0, some].reshape(256, width))
+            raised = transposed_product(nrm[...], wall[1, some].reshape(256, width))
             act[h] = (gated / (1.0 + jnp.exp(-gated)) * raised).astype(BF)
             return carry
 
@@ -536,48 +632,29 @@
             at = pl.ds(pl.multiple_of(n * 512, 512), 512)
             activated = jnp.concatenate([act[0], act[1]], axis=1)
             term = jnp.dot(activated, wall[2, :, :, at].reshape(512, 512), preferred_element_type=F32)
-            part2[row, :, :, at] = term.astype(BF).reshape(8, 32, 512)
+            term = term.astype(BF).reshape(4, 2, 32, 512)
+            for i, k in enumerate(ks):
+                part2[k, :, :, at] = term[i]
             return carry
 
         lax.fori_loop(0, width // 512, columns, 0)
 
-    feed(0)
-    twos[0].cores()
-    ag2.ready(1)
-    feed(1)
-    twos[1].cores()
-    twos[1].first()
-    twos[0].first()
-    twos[1].second()
-    twos[0].second()
-    zsend[...] = twos[1].total().astype(BF)
-    last = links.send(zsend, zrecv, ag2.zm)
-    value = residual[...] + twos[0].total()
-    links.recv(last, zrecv)
-    out[...] = (value + zrecv[...].astype(F32)).astype(BF)
+    feed((7, 0, 1, 2))
+    two.cores((7, 0, 1, 2))
+    ag2.last()
+    ag2.ready((3, 5, 6, 4))
+    feed((3, 4, 5, 6))
+    two.cores((4, 3, 5, 6))
+    two.arrive((7, 0, 1, 2, 4, 3, 5, 6))
+    for k in (4, 3, 2, 1):
+        two.hop(k)
+    for p in (0, 1):
+        at = pl.ds(16 * p, 16)
+        out[at, :] = (residual[at, :] + two.total(p)).astype(BF)
     for handle, region in kv_h:
         links.recv(handle, region)
     own_kv.wait()
     links.drain()
-
-
-def weight_steps(planes):
-    gate, up, down = planes
-
-    def near(plane):
-        return [lambda: plane.y_near(3), lambda: plane.y_near(1)]
-
-    def last(plane):
-        return [plane.y_near_far] + [lambda dz=dz: plane.y_far(dz) for dz in (0, 3, 1, 2)]
-
-    return [
-        [gate.z_near],
-        [up.z_near],
-        [down.z_near] + near(gate),
-        [],
-        [gate.z_far] + near(up) + [up.z_far] + near(down) + [down.z_far],
-        last(gate) + last(up) + last(down),
-    ]
 
 
 def vmem(count):
@@ -635,16 +712,12 @@
         ((2, 16, width), BF),
         ((2, 32, width), BF),
         ((32, width), F32),
-        ((32, width), BF),
-        ((2, 8, 32, width), BF),
+        ((8, 2, 32, width), BF),
         ((2, 256, 256), BF),
-        ((2, 8, 32, width), BF),
-        ((2, 4, 32, width), BF),
-        ((2, 3, 32, width), BF),
-        ((2, 2, 16, width), BF),
-        ((2, 2, 32, width), BF),
-        ((32, width), BF),
-        ((32, width), BF),
+        ((8, 2, 32, width), BF),
+        ((8, 32, width), BF),
+        ((2, 4, 2, 16, width), BF),
+        ((2, 4, 2, 16, width), BF),
     ]
     hidden_out, kv_out = pl.pallas_call(
         layer_kernel,

time: 135 us -> 131 us (0.970); the launches traced: 133 us -> 131 us
  Pallas kernels: 126 us -> 124 us
    pallas_call x1, Pallas kernels: 126 us -> 124 us  [on_device(): pl.pallas_call(layer_kernel, out_shape=[jax.ShapeDtypeStruct((32, width),...]
where the time goes in v4:
time: 131 us
  Pallas kernels  124 us (95%)
  local copies, waits for them, and re-layouts  3.3 us (3%)
  other arithmetic  2.26 us (2%)
  between operations  1.39 us (1%)
    pallas_call x1, Pallas kernels, on_device(): pl.pallas_call(layer_kernel, out_shape=[jax.ShapeDtypeStruct((32, width),...  124 us

profile of v4, /device:TPU:8, one launch (start us, length us, event | category | flops | bytes accessed | tf_op | source)
XLA Modules:
  0.0 130.9 jit_solution(144099399751423135)
XLA Ops:
  1.3 0.5 fusion
  1.9 0.0 copy-start.2
  1.9 1.0 pad_maximum_fusion
  2.9 0.0 copy-start
  2.9 0.0 copy-done.2
  2.9 0.1 select_reduce_fusion
  3.0 0.1 mul.48
  3.1 0.1 add.74
  3.2 0.1 add.75
  3.3 0.1 add.77
  3.4 0.6 fusion.1
  4.0 0.0 copy-done
  4.0 0.7 copy.22
  4.7 124.0 %layer.1 = (bf16[32,2048]{1,0:T(8,128)(2,1)}, bf16[8,32,128]{2,1,0:T(8,128)(2,1)}) custom-call(bf16[32,2048]{1,0:T(8,128)(2,1)} %bitcast.27, bf16[8,128,128]{2,1,0:T(8,128)(2,1)} %bitcast.23, bf16[2,32,2048]{2,1,0:T(8,128)(2,1)} %bitcast.25, bf16[32,2048]{1,0:T(8,128)(2,1)} %wkv.1, bf16[64,2048]{1,0:T(8,128)(2,1)} %wo.1, bf16[32,2048]{1,0:T(8,128)(2,1)} %gate.1, ...), custom_call_target="tpu_custom_call" | custom-call | tf_op jit(solution)/shard_map/layer/pallas_call | solution.py:722
  128.7 0.0 copy-start.1
  128.7 1.5 %copy.25 = bf16[1,32,8,128]{3,2,1,0:T(8,128)(2,1)} copy(bf16[1,32,8,128]{3,1,2,0:T(8,128)(2,1)} %bitcast.29) | data formatting | bytes 131072
  130.2 0.0 copy-done.1
  130.3 0.7 copy.28
  (5 shorter events, 0.0 us)
Async XLA Ops:
  1.9 1.0 copy-start.2
  2.9 1.2 copy-start
  128.7 1.5 %copy-start.1 = (bf16[32,2048]{1,0:T(8,128)(2,1)S(1)}, bf16[32,2048]{1,0:T(8,128)(2,1)}, u32[]{:S(2)}) copy-start(bf16[32,2048]{1,0:T(8,128)(2,1)} %get-tuple-element.4) | copy-start | bytes 393220

commit v5 on v4

--- a/solution.py
+++ b/solution.py
@@ -214,40 +214,50 @@
             self.xs = [{"dev": dev_of(zh, (x + s) % 4, c)} for s in (1, 3)]
         self.mate = {"dev": dev_of(zh, x, 1 - c)}
         self.dx = (2, 1, 3, 0)
+        self.ch, self.x1, self.x2 = {}, [], []
 
     def block(self, k, other=False):
         return ((self.x + self.dx[k]) % 4) * 2 + (1 - self.c if other else self.c)
 
-    def cores(self):
-        self.ch = [self.l.send(self.part.at[self.block(k, True)], self.rc.at[k], self.mate) for k in range(4)]
-
-    def pair_sum(self, k):
+    def cores(self, ks):
+        for k in ks:
+            self.ch[k] = self.l.send(self.part.at[self.block(k, True)], self.rc.at[k], self.mate)
+
+    def arrive(self, k):
         self.l.recv(self.ch[k], self.rc.at[k])
-        return self.part[self.block(k)].astype(F32) + self.rc[k].astype(F32)
+
+    def own(self, k, at):
+        return self.part[self.block(k), at].astype(F32) + self.rc[k, at].astype(F32)
 
     def first(self):
-        self.q[0] = self.pair_sum(0).astype(BF)
-        pieces = halves(self.q, 0)
-        self.x1 = [self.l.send(pieces[s], self.xh.at[s], self.xs[s]) for s in (0, 1)]
+        self.arrive(0)
+        for s in (0, 1):
+            at = pl.ds(16 * s, 16)
+            self.q[0, at] = self.own(0, at).astype(BF)
+            self.x1.append(self.l.send(self.q.at[0, at], self.xh.at[s], self.xs[s]))
+
+    def push(self, s, q, more=None):
+        at = pl.ds(16 * q, 16)
+        value = self.own(1 + s, at)
+        if more is not None:
+            value = value + more
+        self.q[1 + s, at] = value.astype(BF)
+        self.x2.append((self.l.send(self.q.at[1 + s, at], self.xf.at[s, at], self.xs[s]), self.xf.at[s, at]))
 
     def second(self):
-        self.x2 = []
         for s in (0, 1):
-            value = self.pair_sum(1 + s)
+            self.arrive(1 + s)
+            self.push(s, 1 - s)
+        for s in (0, 1):
             self.l.recv(self.x1[s], self.xh.at[s])
-            arrived = self.xh[s].astype(F32)
-            top = value[:16] + arrived if s == 0 else value[:16]
-            low = value[16:] + arrived if s == 1 else value[16:]
-            self.q[1 + s, pl.ds(0, 16)] = top.astype(BF)
-            self.q[1 + s, pl.ds(16, 16)] = low.astype(BF)
-            self.x2.append(self.l.send(self.q.at[1 + s], self.xf.at[s], self.xs[s]))
+            self.push(s, s, self.xh[s].astype(F32))
 
     def total(self):
-        value = self.pair_sum(3)
-        for s in (0, 1):
-            self.l.recv(self.x2[s], self.xf.at[s])
-            value = value + self.xf[s].astype(F32)
-        return value
+        self.arrive(3)
+        value = self.own(3, pl.ds(0, 32))
+        for handle, region in self.x2:
+            self.l.recv(handle, region)
+        return value + self.xf[0].astype(F32) + self.xf[1].astype(F32)
 
 
 def z_neighbours():
@@ -328,7 +338,7 @@
     def hop(self, k):
         for p in (0, 1):
             for s in (0, 1):
-                q = p if s == 0 else 1 - p
+                q = 1 - s if p == 0 else s
                 if k == 4 and q != s:
                     continue
                 value = self.own(k if s == 0 else -k, q)
@@ -386,6 +396,16 @@
         links, x, xs, lambda j: wkv_all.at[j * 2 + c, :, quarter(y)],
         lambda j, s: wkv_all.at[j * 2 + c, pl.ds(16 * s, 16), quarter(y)], wkv.at[:, quarter(y)],
     )
+    o_ring = Ring(
+        links, x, xs, lambda j: wo_all.at[j, pl.ds(64, 64), quarter(y)],
+        lambda j, s: wo_all.at[j, pl.ds(64 + 32 * s, 32), quarter(y)], wo.at[:, quarter(y)],
+    )
+    o_rings = {}
+    for dx in (1, 2, 3):
+        o_rings[dx] = Ring(
+            links, y, ys, lambda k, j=(x + dx) % 4: wo_all.at[j, pl.ds(64, 64), quarter(k)],
+            lambda k, s, j=(x + dx) % 4: wo_all.at[j, pl.ds(64 + 32 * s, 32), quarter(k)],
+        )
     y_rings = {}
     for dx in (1, 2, 3):
         j = (x + dx) % 4
@@ -403,9 +423,6 @@
         links, x, xs, lambda j: kv_all.at[:, j * 2 + c], lambda j, s: kv_all.at[s, j * 2 + c],
         None, mate, lambda j: kv_all.at[:, j * 2 + 1 - c],
     )
-    o_ring = Ring(
-        links, x, xs, lambda j: wo_all.at[j, pl.ds(64, 64)], lambda j, s: wo_all.at[j, pl.ds(64 + 32 * s, 32)], wo,
-    )
     new = Ring(
         links, x, xs, lambda j: fresh.at[c, :, j], lambda j, s: fresh.at[c, pl.ds(2 * s, 2), j],
         None, mate, lambda j: fresh.at[1 - c, :, j],
@@ -420,6 +437,7 @@
     kv_ring.start()
     q_ring.start()
     hidden.start()
+    o_ring.start()
     w_core = [(links.send(wkv, wkv_all.at[mine], mate), wkv_all.at[x * 2 + 1 - c])]
     own_planes = [local.copy(own, wall.at[a, x * 4 + y]) for a, own in enumerate((gate, up, down))]
     own_pages = local.copy(pool.at[pl.ds(2 * zh, 2)], kv_all.at[:, mine, zh])
@@ -434,6 +452,7 @@
     for dx in (1, 3):
         for ring in y_rings[dx]:
             ring.start()
+    o_ring.near()
     for copy in own_planes:
         copy.wait()
     a_plane.start_one()
@@ -441,25 +460,26 @@
     q_ring.far()
     for ring in y_rings[2]:
         ring.start()
-    b_plane.start_one()
-    a_plane.start_two()
     far_pages = []
     for s, dz in ((0, 3), (1, 1)):
         links.recv(relayed[s], relay.at[s])
         far_pages.append(links.send(relay.at[s], kv_all.at[s, mine, (zh + dz) % 4], zs[s]))
-    for dx in (1, 3):
+    for dx in (1, 3, 2):
         for ring in y_rings[dx]:
             ring.near()
-    a_plane.near_one()
+    o_ring.far()
+    for dx in (1, 3, 2):
+        o_rings[dx].start()
+    b_plane.start_one()
+    a_plane.start_two()
     for s, dz in ((0, 3), (1, 1)):
         links.recv(near_pages[s], kv_all.at[:, mine, (zh + dz) % 4])
     own_pages.wait()
     for s in (0, 1):
         links.recv(far_pages[s], kv_all.at[s, mine, (zh + 2) % 4])
     pages.start()
-    for ring in y_rings[2]:
-        ring.near()
     hidden.near()
+    a_plane.near_one()
     for k in range(4):
         wo_all[k, pl.ds(0, 64)] = jnp.zeros((64, width), BF)
     for copy in early:
@@ -469,9 +489,12 @@
             ring.far()
         block = (x + dx) % 4 * 2
         w_core.append((links.send(wkv_all.at[block + c], wkv_all.at[block + c], mate), wkv_all.at[block + 1 - c]))
-    a_plane.spread()
+    for dx in (1, 3, 2):
+        o_rings[dx].near()
     hidden.far()
     pages.near()
+    b_plane.near_one()
+    a_plane.spread()
     hidden.ready()
     for handle, region in w_core:
         links.recv(handle, region)
@@ -480,7 +503,7 @@
         nrm[pl.ds(pl.multiple_of(i * 32, 32), 32), :] = root_norm(hid_col[i], gain_one[...])
         return carry
 
-    lax.fori_loop(0, 8, norm, 0)
+    lax.fori_loop(0, 8, norm, 0, unroll=2)
     lane = lax.broadcasted_iota(jnp.int32, (256, 2 * HD), 1)
     first_half = lane % HD < HD // 2
 
@@ -504,13 +527,7 @@
         for i in (0, 1):
             head = turned if i == 0 else pltpu.roll(turned, 64, 1)
             q_all[k, :, i] = jnp.where(lane < HD, head, 0.0).astype(BF).reshape(4, 64, 128)
-    new.near()
-    o_ring.start()
     pages.far()
-    new.far()
-    a_plane.far_one()
-    b_plane.near_one()
-    new.ready()
     pages.ready()
 
     prefix = 4096
@@ -521,32 +538,37 @@
             running = jnp.maximum(running, scores[:, k * 128 : (k + 1) * 128])
         return running
 
-    def attend(k, p):
-        q = q_all[k, 2 * p : 2 * p + 2].reshape(QT, 2 * HD)
-
-        def keys_at(i):
-            return kv_all[k, pl.ds(i * per_block, per_block)].reshape(KC, 2 * HD)
+    def keys_at(k, i):
+        return kv_all[k, pl.ds(i * per_block, per_block)].reshape(KC, 2 * HD)
+
+    def queries_of(k, p):
+        return q_all[k, pl.ds(2 * p, 2)].reshape(QT, 2 * HD)
+
+    def score(k, p):
+        q = queries_of(k, p)
 
         def score_prefix(i, running):
             at = pl.ds(pl.multiple_of(i * KC, KC), KC)
-            scores = transposed_product(q, keys_at(i)) + bias[:, at]
-            s_ref[:, at] = scores
+            scores = transposed_product(q, keys_at(k, i)) + bias[:, at]
+            s_ref[k, :, at] = scores
             return lanes_max(running, scores)
 
-        running = lax.fori_loop(0, prefix // KC, score_prefix, jnp.full((QT, 128), MASKED, F32), unroll=2)
-        row = lax.broadcasted_iota(jnp.int32, (QT, 256), 0)
+        return lax.fori_loop(0, prefix // KC, score_prefix, jnp.full((QT, 128), MASKED, F32), unroll=True)
+
+    def attend(k, p, running):
+        q = queries_of(k, p)
+        row = lax.broadcasted_iota(jnp.int32, (QT, KC), 0)
         token = (2 * p + row // 128) * 256 + x * 64 + row % 64
-        col = lax.broadcasted_iota(jnp.int32, (QT, 256), 1)
-        for i in range(2 * p + 2):
-            scores = transposed_product(q, fresh[k, i].reshape(256, 2 * HD))
-            scores = jnp.where(col + i * 256 <= token, scores, MASKED)
-            s_ref[:, prefix + i * 256 : prefix + (i + 1) * 256] = scores
-            running = lanes_max(running, scores)
+        col = lax.broadcasted_iota(jnp.int32, (QT, KC), 1)
+        added = fresh[k].reshape(KC, 2 * HD)
+        scores = jnp.where(col <= token, transposed_product(q, added), MASKED)
+        s_ref[k, :, pl.ds(prefix, KC)] = scores
+        running = lanes_max(running, scores)
         top = jnp.broadcast_to(jnp.max(running, axis=1, keepdims=True), (QT, 128))
 
         def weigh(at, keys, carried):
             total, summed = carried
-            scores = s_ref[:, at]
+            scores = s_ref[k, :, at]
             pieces = []
             for n in range(scores.shape[1] // 128):
                 weights = jnp.exp(scores[:, n * 128 : (n + 1) * 128] - top)
@@ -556,62 +578,73 @@
             return total, summed + jnp.dot(weights, keys, preferred_element_type=F32)
 
         def weigh_prefix(i, carried):
-            return weigh(pl.ds(pl.multiple_of(i * KC, KC), KC), keys_at(i), carried)
+            return weigh(pl.ds(pl.multiple_of(i * KC, KC), KC), keys_at(k, i), carried)
 
         carried = (jnp.zeros((QT, 128), F32), jnp.zeros((QT, 2 * HD), F32))
-        carried = lax.fori_loop(0, prefix // KC, weigh_prefix, carried, unroll=2)
-        for i in range(2 * p + 2):
-            carried = weigh(pl.ds(prefix + i * 256, 256), fresh[k, i].reshape(256, 2 * HD), carried)
-        total, summed = carried
+        carried = lax.fori_loop(0, prefix // KC, weigh_prefix, carried, unroll=True)
+        total, summed = weigh(pl.ds(prefix, KC), added, carried)
         mixed = (summed / jnp.sum(total, axis=1, keepdims=True)).astype(BF).reshape(2, 2, 64, 128)
         for z in (0, 1):
             for i in (0, 1):
-                att[2 * k + i, (2 * p + z) * 64 : (2 * p + z + 1) * 64] = mixed[z, i]
-
-    attend(0, 0)
-    o_ring.near()
+                att[2 * k + i, pl.ds(pl.multiple_of((2 * p + z) * 64, 64), 64)] = mixed[z, i]
+
+    one = RowScatter(links, part1, rc1, q1, xh1, xf1, True)
+
+    def out_project(p):
+        tokens = pl.ds(pl.multiple_of(p * 128, 128), 128)
+
+        def columns(n, carry):
+            at = pl.ds(pl.multiple_of(n * 512, 512), 512)
+            term = None
+            for k in (0, 2):
+                heads = jnp.concatenate([att[k, tokens], att[k + 1, tokens]], axis=1)
+                product = jnp.dot(heads, wo_all[pl.ds(k, 2), :, at].reshape(256, 512), preferred_element_type=F32)
+                term = product if term is None else term + product
+            part1[pl.ds(4 * p, 4), :, at] = term.astype(BF).reshape(4, 32, 512)
+            return carry
+
+        lax.fori_loop(0, width // 512, columns, 0, unroll=True)
+
+    far_pair, own_pair = 1 - zh // 2, zh // 2
+    running = [score(0, far_pair)]
+    new.near()
+    running.append(score(1, far_pair))
+    new.far()
+    a_plane.far_one()
     b_plane.start_two()
     b_plane.spread()
+    new.ready()
+    attend(0, far_pair, running[0])
+    for dx in (1, 3, 2):
+        o_rings[dx].far()
+    own_wo.wait()
     a_plane.near_two(0)
-    attend(1, 0)
+    attend(1, far_pair, running[1])
+    out_project(far_pair)
+    one.cores((0,))
+    a_plane.near_two(3)
+    attend(0, own_pair, score(0, own_pair))
+    one.first()
     b_plane.far_one()
-    a_plane.near_two(3)
-    attend(0, 1)
-    o_ring.far()
     a_plane.near_two(1)
-    attend(1, 1)
-    own_wo.wait()
-
-    one = RowScatter(links, part1, rc1, q1, xh1, xf1, True)
-
-    def out_columns(n, carry):
-        at = pl.ds(pl.multiple_of(n * 512, 512), 512)
-        term = None
-        for k in (0, 2):
-            heads = jnp.concatenate([att[k], att[k + 1]], axis=1)
-            product = jnp.dot(heads, wo_all[pl.ds(k, 2), :, at].reshape(256, 512), preferred_element_type=F32)
-            term = product if term is None else term + product
-        part1[:, :, at] = term.astype(BF).reshape(8, 32, 512)
-        return carry
-
-    lax.fori_loop(0, width // 512, out_columns, 0)
-    one.cores()
-    one.first()
+    b_plane.near_two(0)
+    attend(1, own_pair, score(1, own_pair))
+    out_project(own_pair)
+    one.cores((1, 2, 3))
     one.second()
     residual[...] = one.total() + hid[...].astype(F32)
     rows[0, 0] = root_norm(residual[...], gain_two[...])
     ag2.start()
+    b_plane.near_two(3)
+    b_plane.near_two(1)
     a_plane.near_two_far()
-    b_plane.near_two(0)
     ag2.hop(1)
+    b_plane.near_two_far()
     ag2.hop(2)
     ag2.hop(3)
-    b_plane.near_two(3)
-    b_plane.near_two(1)
-    b_plane.near_two_far()
     a_plane.far_two()
+    b_plane.far_two()
     ag2.ready((0, 1, 7, 2))
-    b_plane.far_two()
 
     two = ColumnScatter(links, part2, rc2, q2, arrived2)
 
@@ -626,7 +659,7 @@
             act[h] = (gated / (1.0 + jnp.exp(-gated)) * raised).astype(BF)
             return carry
 
-        lax.fori_loop(0, 2, units, 0)
+        lax.fori_loop(0, 2, units, 0, unroll=True)
 
         def columns(n, carry):
             at = pl.ds(pl.multiple_of(n * 512, 512), 512)
@@ -637,7 +670,7 @@
                 part2[k, :, :, at] = term[i]
             return carry
 
-        lax.fori_loop(0, width // 512, columns, 0)
+        lax.fori_loop(0, width // 512, columns, 0, unroll=True)
 
     feed((7, 0, 1, 2))
     two.cores((7, 0, 1, 2))
@@ -704,7 +737,7 @@
         ((256, width), BF),
         ((2, 4, 2, 64, 2 * HD), BF),
         ((2, 4, 4, 64, 2 * HD), BF),
-        ((QT, 32 * slots + tokens), F32),
+        ((2, QT, 32 * slots + tokens), F32),
         ((4, 256, 2 * HD), BF),
         ((8, 32, width), BF),
         ((4, 32, width), BF),

time: 131 us -> 114 us (0.87)
  Pallas kernels: 124 us -> 107 us
    pallas_call x1, Pallas kernels: 124 us -> 107 us  [on_device(): pl.pallas_call(layer_kernel, out_shape=[jax.ShapeDtypeStruct((32, width),...]
where the time goes in v5:
time: 114 us
  Pallas kernels  107 us (94%)
  local copies, waits for them, and re-layouts  3.3 us (3%)
  other arithmetic  2.26 us (2%)
  between operations  1.39 us (1%)
    pallas_call x1, Pallas kernels, on_device(): pl.pallas_call(layer_kernel, out_shape=[jax.ShapeDtypeStruct((32, width),...  107 us

profile of v5, /device:TPU:8, one launch (start us, length us, event | category | flops | bytes accessed | tf_op | source)
XLA Modules:
  0.0 113.6 jit_solution(4985338607123323853)
XLA Ops:
  1.3 0.5 fusion
  1.9 0.0 copy-start.2
  1.9 1.0 pad_maximum_fusion
  2.9 0.0 copy-start
  2.9 0.0 copy-done.2
  2.9 0.1 select_reduce_fusion
  3.0 0.1 mul.48
  3.1 0.1 add.74
  3.2 0.1 add.75
  3.3 0.1 add.77
  3.4 0.6 fusion.1
  4.0 0.0 copy-done
  4.0 0.7 copy.22
  4.7 106.6 %layer.1 = (bf16[32,2048]{1,0:T(8,128)(2,1)}, bf16[8,32,128]{2,1,0:T(8,128)(2,1)}) custom-call(bf16[32,2048]{1,0:T(8,128)(2,1)} %bitcast.27, bf16[8,128,128]{2,1,0:T(8,128)(2,1)} %bitcast.23, bf16[2,32,2048]{2,1,0:T(8,128)(2,1)} %bitcast.25, bf16[32,2048]{1,0:T(8,128)(2,1)} %wkv.1, bf16[64,2048]{1,0:T(8,128)(2,1)} %wo.1, bf16[32,2048]{1,0:T(8,128)(2,1)} %gate.1, ...), custom_call_target="tpu_custom_call" | custom-call | tf_op jit(solution)/shard_map/layer/pallas_call | solution.py:755
  111.4 0.0 copy-start.1
  111.4 1.5 %copy.25 = bf16[1,32,8,128]{3,2,1,0:T(8,128)(2,1)} copy(bf16[1,32,8,128]{3,1,2,0:T(8,128)(2,1)} %bitcast.29) | data formatting | bytes 131072
  112.9 0.0 copy-done.1
  112.9 0.7 copy.28
  (5 shorter events, 0.0 us)
Async XLA Ops:
  1.9 1.0 copy-start.2
  2.9 1.2 %copy-start = (bf16[1,8,16,8,128]{4,3,2,1,0:T(8,128)(2,1)S(1)}, bf16[1,8,16,8,128]{4,3,2,1,0:T(8,128)(2,1)}, u32[]{:S(2)}) copy-start(bf16[1,8,16,8,128]{4,3,2,1,0:T(8,128)(2,1)} %param.21) | copy-start | bytes 786436
  111.4 1.5 %copy-start.1 = (bf16[32,2048]{1,0:T(8,128)(2,1)S(1)}, bf16[32,2048]{1,0:T(8,128)(2,1)}, u32[]{:S(2)}) copy-start(bf16[32,2048]{1,0:T(8,128)(2,1)} %get-tuple-element.4) | copy-start | bytes 393220

commit v6 on v5

--- a/solution.py
+++ b/solution.py
@@ -362,7 +362,7 @@
     hid, pool, wq, wkv, wo, gate, up, down, gain_one, gain_two, cosine, sine, bias,
     out, kv_out,
     hid_col, relay, kv_all, wq_all, wkv_all, wo_all, wall, nrm, q_all, fresh, s_ref, att,
-    part1, rc1, q1, xh1, xf1, residual, rows, act, part2, rc2, q2, arrived2,
+    part1, rc1, q1, xh1, xf1, residual, rows, act, part2, rc2, q2, arrived2, kv_got,
     send_sems, recv_sems, local_sems,
 ):
     zh, x, c = place()
@@ -430,13 +430,13 @@
     greet(list(column.values()) + xs + ag2.tos + ys)
 
     mine = x * 2 + c
-    near_pages, relayed = [], []
+    near_pages, relayed, far_pages = [], [], []
+    for s in (0, 1):
+        relayed.append(links.send(pool.at[2 * ((zh + 2) % 4) + s], relay.at[s], zs[s]))
     for s, dz in ((0, 1), (1, 3)):
         near_pages.append(links.send(pool.at[pl.ds(2 * ((zh + dz) % 4), 2)], kv_all.at[:, mine, zh], zs[s]))
-        relayed.append(links.send(pool.at[2 * ((zh + 2) % 4) + s], relay.at[s], zs[s]))
     kv_ring.start()
     q_ring.start()
-    hidden.start()
     o_ring.start()
     w_core = [(links.send(wkv, wkv_all.at[mine], mate), wkv_all.at[x * 2 + 1 - c])]
     own_planes = [local.copy(own, wall.at[a, x * 4 + y]) for a, own in enumerate((gate, up, down))]
@@ -448,6 +448,10 @@
     ]
     own_wo = local.copy(wo, wo_all.at[x, pl.ds(64, 64)])
     kv_ring.near()
+    for s, dz in ((0, 3), (1, 1)):
+        links.recv(relayed[s], relay.at[s])
+        far_pages.append(links.send(relay.at[s], kv_all.at[s, mine, (zh + dz) % 4], zs[s]))
+    hidden.start()
     q_ring.near()
     for dx in (1, 3):
         for ring in y_rings[dx]:
@@ -460,10 +464,12 @@
     q_ring.far()
     for ring in y_rings[2]:
         ring.start()
-    far_pages = []
     for s, dz in ((0, 3), (1, 1)):
-        links.recv(relayed[s], relay.at[s])
-        far_pages.append(links.send(relay.at[s], kv_all.at[s, mine, (zh + dz) % 4], zs[s]))
+        links.recv(near_pages[s], kv_all.at[:, mine, (zh + dz) % 4])
+    own_pages.wait()
+    for s in (0, 1):
+        links.recv(far_pages[s], kv_all.at[s, mine, (zh + 2) % 4])
+    pages.start()
     for dx in (1, 3, 2):
         for ring in y_rings[dx]:
             ring.near()
@@ -472,29 +478,19 @@
         o_rings[dx].start()
     b_plane.start_one()
     a_plane.start_two()
-    for s, dz in ((0, 3), (1, 1)):
-        links.recv(near_pages[s], kv_all.at[:, mine, (zh + dz) % 4])
-    own_pages.wait()
-    for s in (0, 1):
-        links.recv(far_pages[s], kv_all.at[s, mine, (zh + 2) % 4])
-    pages.start()
-    hidden.near()
     a_plane.near_one()
     for k in range(4):
         wo_all[k, pl.ds(0, 64)] = jnp.zeros((64, width), BF)
     for copy in early:
         copy.wait()
+    hidden.near()
+    pages.near()
     for dx in (1, 3, 2):
         for ring in y_rings[dx]:
             ring.far()
         block = (x + dx) % 4 * 2
         w_core.append((links.send(wkv_all.at[block + c], wkv_all.at[block + c], mate), wkv_all.at[block + 1 - c]))
-    for dx in (1, 3, 2):
-        o_rings[dx].near()
     hidden.far()
-    pages.near()
-    b_plane.near_one()
-    a_plane.spread()
     hidden.ready()
     for handle, region in w_core:
         links.recv(handle, region)
@@ -519,8 +515,8 @@
     kv_h = []
     for (dz, dc), to in column.items():
         src = fresh.at[c, (zh + dz) % 4, x, pl.ds(32 * ((c + dc) % 2), 32)]
-        kv_h.append((links.send(src, kv_out.at[2 * zh + c], to), kv_out.at[2 * ((zh + 4 - dz) % 4) + (c + dc) % 2]))
-    own_kv = local.copy(fresh.at[c, zh, x, pl.ds(32 * c, 32)], kv_out.at[2 * zh + c])
+        kv_h.append((links.send(src, kv_got.at[2 * zh + c], to), kv_got.at[2 * ((zh + 4 - dz) % 4) + (c + dc) % 2]))
+    own_kv = local.copy(fresh.at[c, zh, x, pl.ds(32 * c, 32)], kv_got.at[2 * zh + c])
     queries = transposed_product(nrm[...], wq_all[...].reshape(256, width))
     for k in (0, 1):
         turned = rotate(queries[:, k * 128 : (k + 1) * 128]) * ATTENTION_SCALE
@@ -528,6 +524,9 @@
             head = turned if i == 0 else pltpu.roll(turned, 64, 1)
             q_all[k, :, i] = jnp.where(lane < HD, head, 0.0).astype(BF).reshape(4, 64, 128)
     pages.far()
+    for dx in (1, 3, 2):
+        o_rings[dx].near()
+    a_plane.spread()
     pages.ready()
 
     prefix = 4096
@@ -606,10 +605,11 @@
         lax.fori_loop(0, width // 512, columns, 0, unroll=True)
 
     far_pair, own_pair = 1 - zh // 2, zh // 2
+    new.near()
     running = [score(0, far_pair)]
-    new.near()
+    new.far()
+    b_plane.near_one()
     running.append(score(1, far_pair))
-    new.far()
     a_plane.far_one()
     b_plane.start_two()
     b_plane.spread()
@@ -625,13 +625,13 @@
     a_plane.near_two(3)
     attend(0, own_pair, score(0, own_pair))
     one.first()
-    b_plane.far_one()
     a_plane.near_two(1)
     b_plane.near_two(0)
     attend(1, own_pair, score(1, own_pair))
     out_project(own_pair)
     one.cores((1, 2, 3))
     one.second()
+    b_plane.far_one()
     residual[...] = one.total() + hid[...].astype(F32)
     rows[0, 0] = root_norm(residual[...], gain_two[...])
     ag2.start()
@@ -678,15 +678,17 @@
     ag2.ready((3, 5, 6, 4))
     feed((3, 4, 5, 6))
     two.cores((4, 3, 5, 6))
-    two.arrive((7, 0, 1, 2, 4, 3, 5, 6))
-    for k in (4, 3, 2, 1):
+    for k, blocks in ((4, (4,)), (3, (3, 5)), (2, (2, 6)), (1, (1, 7))):
+        two.arrive(blocks)
         two.hop(k)
+    for handle, region in kv_h:
+        links.recv(handle, region)
+    own_kv.wait()
+    kv_out[...] = jnp.swapaxes(kv_got[...].astype(F32), 0, 1).astype(BF)
+    two.arrive((0,))
     for p in (0, 1):
         at = pl.ds(16 * p, 16)
         out[at, :] = (residual[at, :] + two.total(p)).astype(BF)
-    for handle, region in kv_h:
-        links.recv(handle, region)
-    own_kv.wait()
     links.drain()
 
 
@@ -751,10 +753,11 @@
         ((8, 32, width), BF),
         ((2, 4, 2, 16, width), BF),
         ((2, 4, 2, 16, width), BF),
+        ((KVH, 32, 2 * HD), BF),
     ]
     hidden_out, kv_out = pl.pallas_call(
         layer_kernel,
-        out_shape=[jax.ShapeDtypeStruct((32, width), BF), jax.ShapeDtypeStruct((8, 32, 2 * HD), BF)],
+        out_shape=[jax.ShapeDtypeStruct((32, width), BF), jax.ShapeDtypeStruct((32, 8, 2 * HD), BF)],
         in_specs=vmem(13),
         out_specs=vmem(2),
         scratch_shapes=[pltpu.VMEM(*b) for b in buffers] + [
@@ -769,7 +772,7 @@
         gate_weight, up_weight, down_weight,
         attention_gain.reshape(1, width), feedforward_gain.reshape(1, width), cosine, sine, bias,
     )
-    return hidden_out[None], kv_out.transpose(1, 0, 2)[None]
+    return hidden_out[None], kv_out[None]
 
 
 COPIES = 230

time: 114 us -> 111 us (0.974)
  Pallas kernels: 107 us -> 103 us
    pallas_call x1, Pallas kernels: 107 us -> 103 us  [on_device(): pl.pallas_call(layer_kernel, out_shape=[jax.ShapeDtypeStruct((32, width),...]
where the time goes in v6:
time: 111 us; the launch traced here: 110 us
  Pallas kernels  103 us (93%)
  local copies, waits for them, and re-layouts  3.35 us (3%)
  other arithmetic  2.26 us (2%)
  between operations  1.39 us (1%)
    pallas_call x1, Pallas kernels, on_device(): pl.pallas_call(layer_kernel, out_shape=[jax.ShapeDtypeStruct((32, width),...  103 us
    unnamed x8, local copies, waits for them, and re-layouts  2.24 us

profile of v6, /device:TPU:8, one launch (start us, length us, event | category | flops | bytes accessed | tf_op | source)
XLA Modules:
  0.0 109.8 jit_solution(17234330535920868880)
XLA Ops:
  1.3 0.5 fusion
  1.9 0.0 copy-start.2
  1.9 1.0 pad_maximum_fusion
  2.9 0.0 copy-start
  2.9 0.0 copy-done.2
  2.9 0.1 select_reduce_fusion
  3.0 0.1 mul.48
  3.1 0.1 add.74
  3.2 0.1 add.75
  3.3 0.1 add.77
  3.4 0.6 fusion.1
  4.0 0.0 copy-done
  4.0 0.7 copy.19
  4.7 102.8 %layer.1 = (bf16[32,2048]{1,0:T(8,128)(2,1)}, bf16[32,8,128]{2,1,0:T(8,128)(2,1)}) custom-call(bf16[32,2048]{1,0:T(8,128)(2,1)} %bitcast.25, bf16[8,128,128]{2,1,0:T(8,128)(2,1)} %bitcast.21, bf16[2,32,2048]{2,1,0:T(8,128)(2,1)} %bitcast.23, bf16[32,2048]{1,0:T(8,128)(2,1)} %wkv.1, bf16[64,2048]{1,0:T(8,128)(2,1)} %wo.1, bf16[32,2048]{1,0:T(8,128)(2,1)} %gate.1, ...), custom_call_target="tpu_custom_call" | custom-call | tf_op jit(solution)/shard_map/layer/pallas_call | solution.py:758
  107.5 0.0 copy-start.1
  107.6 1.6 %copy.25 = bf16[1,32,2048]{2,1,0:T(8,128)(2,1)} copy(bf16[1,32,2048]{2,1,0:T(8,128)(2,1)} %bitcast.24) | data formatting | bytes 262144
  109.2 0.0 copy-done.1
  109.2 0.6 copy.26
  (5 shorter events, 0.0 us)
Async XLA Ops:
  1.9 1.0 copy-start.2
  2.9 1.2 %copy-start = (bf16[1,8,16,8,128]{4,3,2,1,0:T(8,128)(2,1)S(1)}, bf16[1,8,16,8,128]{4,3,2,1,0:T(8,128)(2,1)}, u32[]{:S(2)}) copy-start(bf16[1,8,16,8,128]{4,3,2,1,0:T(8,128)(2,1)} %param.21) | copy-start | bytes 786436
  107.5 1.6 %copy-start.1 = (bf16[32,8,128]{2,1,0:T(8,128)(2,1)S(1)}, bf16[32,8,128]{2,1,0:T(8,128)(2,1)}, u32[]{:S(2)}) copy-start(bf16[32,8,128]{2,1,0:T(8,128)(2,1)} %get-tuple-element.5) | copy-start | bytes 196612

commit v7 on v6

--- a/solution.py
+++ b/solution.py
@@ -362,7 +362,7 @@
     hid, pool, wq, wkv, wo, gate, up, down, gain_one, gain_two, cosine, sine, bias,
     out, kv_out,
     hid_col, relay, kv_all, wq_all, wkv_all, wo_all, wall, nrm, q_all, fresh, s_ref, att,
-    part1, rc1, q1, xh1, xf1, residual, rows, act, part2, rc2, q2, arrived2, kv_got,
+    part1, rc1, q1, xh1, xf1, residual, rows, act, part2, rc2, q2, arrived2, kv_got, kv_relay,
     send_sems, recv_sems, local_sems,
 ):
     zh, x, c = place()
@@ -427,7 +427,7 @@
         links, x, xs, lambda j: fresh.at[c, :, j], lambda j, s: fresh.at[c, pl.ds(2 * s, 2), j],
         None, mate, lambda j: fresh.at[1 - c, :, j],
     )
-    greet(list(column.values()) + xs + ag2.tos + ys)
+    greet([to for (dz, dc), to in column.items() if dz != 2] + xs + ag2.tos + ys)
 
     mine = x * 2 + c
     near_pages, relayed, far_pages = [], [], []
@@ -484,6 +484,15 @@
     for copy in early:
         copy.wait()
     hidden.near()
+
+    def norm(dz):
+        for core in (0, 1):
+            block = (zh + dz) % 4 * 2 + core
+            nrm[pl.ds(pl.multiple_of(block * 32, 32), 32), :] = root_norm(hid_col[block], gain_one[...])
+
+    for n, dz in enumerate((0, 3, 1)):
+        links.recv(*hidden.waits[n])
+        norm(dz)
     pages.near()
     for dx in (1, 3, 2):
         for ring in y_rings[dx]:
@@ -491,15 +500,11 @@
         block = (x + dx) % 4 * 2
         w_core.append((links.send(wkv_all.at[block + c], wkv_all.at[block + c], mate), wkv_all.at[block + 1 - c]))
     hidden.far()
-    hidden.ready()
+    links.recv(*hidden.waits[3])
     for handle, region in w_core:
         links.recv(handle, region)
 
-    def norm(i, carry):
-        nrm[pl.ds(pl.multiple_of(i * 32, 32), 32), :] = root_norm(hid_col[i], gain_one[...])
-        return carry
-
-    lax.fori_loop(0, 8, norm, 0, unroll=2)
+    norm(2)
     lane = lax.broadcasted_iota(jnp.int32, (256, 2 * HD), 1)
     first_half = lane % HD < HD // 2
 
@@ -512,10 +517,14 @@
         pairs = keyvals[:, k * 128 : (k + 1) * 128].astype(F32)
         fresh[k, :, x] = jnp.where(lane < HD, rotate(pairs), pairs).astype(BF).reshape(4, 64, 128)
     new.start(False)
-    kv_h = []
+    kv_h, kv_far = [], []
     for (dz, dc), to in column.items():
         src = fresh.at[c, (zh + dz) % 4, x, pl.ds(32 * ((c + dc) % 2), 32)]
-        kv_h.append((links.send(src, kv_got.at[2 * zh + c], to), kv_got.at[2 * ((zh + 4 - dz) % 4) + (c + dc) % 2]))
+        if dz == 2:
+            kv_far.append(links.send(src, kv_relay.at[dc], column[1, 0]))
+        else:
+            region = kv_got.at[2 * ((zh + 4 - dz) % 4) + (c + dc) % 2]
+            kv_h.append((links.send(src, kv_got.at[2 * zh + c], to), region))
     own_kv = local.copy(fresh.at[c, zh, x, pl.ds(32 * c, 32)], kv_got.at[2 * zh + c])
     queries = transposed_product(nrm[...], wq_all[...].reshape(256, width))
     for k in (0, 1):
@@ -607,9 +616,13 @@
     far_pair, own_pair = 1 - zh // 2, zh // 2
     new.near()
     running = [score(0, far_pair)]
-    new.far()
     b_plane.near_one()
     running.append(score(1, far_pair))
+    new.far()
+    for dc in (0, 1):
+        links.recv(kv_far[dc], kv_relay.at[dc])
+        onward = links.send(kv_relay.at[dc], kv_got.at[2 * ((zh + 3) % 4) + c], column[1, dc])
+        kv_h.append((onward, kv_got.at[2 * ((zh + 2) % 4) + (c + dc) % 2]))
     a_plane.far_one()
     b_plane.start_two()
     b_plane.spread()
@@ -754,6 +767,7 @@
         ((2, 4, 2, 16, width), BF),
         ((2, 4, 2, 16, width), BF),
         ((KVH, 32, 2 * HD), BF),
+        ((2, 32, 2 * HD), BF),
     ]
     hidden_out, kv_out = pl.pallas_call(
         layer_kernel,

time: 111 us -> 110 us (level)
  no operation moved by 1% of the time
where the time goes in v7:
time: 110 us; the launch traced here: 109 us
  Pallas kernels  102 us (93%)
  local copies, waits for them, and re-layouts  3.35 us (3%)
  other arithmetic  2.26 us (2%)
  between operations  1.39 us (1%)
    pallas_call x1, Pallas kernels, on_device(): pl.pallas_call(layer_kernel, out_shape=[jax.ShapeDtypeStruct((32, width),...  102 us
    unnamed x8, local copies, waits for them, and re-layouts  2.24 us

profile of v7, /device:TPU:8, one launch (start us, length us, event | category | flops | bytes accessed | tf_op | source)
XLA Modules:
  0.0 109.2 jit_solution(18288546144648784641)
XLA Ops:
  1.3 0.5 fusion
  1.9 0.0 copy-start.2
  1.9 1.0 pad_maximum_fusion
  2.9 0.0 copy-start
  2.9 0.0 copy-done.2
  2.9 0.1 select_reduce_fusion
  3.0 0.1 mul.48
  3.1 0.1 add.74
  3.2 0.1 add.75
  3.3 0.1 add.77
  3.4 0.6 fusion.1
  4.0 0.0 copy-done
  4.0 0.7 copy.19
  4.7 102.2 %layer.1 = (bf16[32,2048]{1,0:T(8,128)(2,1)}, bf16[32,8,128]{2,1,0:T(8,128)(2,1)}) custom-call(bf16[32,2048]{1,0:T(8,128)(2,1)} %bitcast.25, bf16[8,128,128]{2,1,0:T(8,128)(2,1)} %bitcast.21, bf16[2,32,2048]{2,1,0:T(8,128)(2,1)} %bitcast.23, bf16[32,2048]{1,0:T(8,128)(2,1)} %wkv.1, bf16[64,2048]{1,0:T(8,128)(2,1)} %wo.1, bf16[32,2048]{1,0:T(8,128)(2,1)} %gate.1, ...), custom_call_target="tpu_custom_call" | custom-call | tf_op jit(solution)/shard_map/layer/pallas_call | solution.py:772
  107.0 0.0 copy-start.1
  107.0 1.6 %copy.25 = bf16[1,32,2048]{2,1,0:T(8,128)(2,1)} copy(bf16[1,32,2048]{2,1,0:T(8,128)(2,1)} %bitcast.24) | data formatting | bytes 262144
  108.6 0.0 copy-done.1
  108.6 0.6 copy.26
  (5 shorter events, 0.0 us)
Async XLA Ops:
  1.9 1.0 copy-start.2
  2.9 1.2 %copy-start = (bf16[1,8,16,8,128]{4,3,2,1,0:T(8,128)(2,1)S(1)}, bf16[1,8,16,8,128]{4,3,2,1,0:T(8,128)(2,1)}, u32[]{:S(2)}) copy-start(bf16[1,8,16,8,128]{4,3,2,1,0:T(8,128)(2,1)} %param.21) | copy-start | bytes 786436
  107.0 1.6 %copy-start.1 = (bf16[32,8,128]{2,1,0:T(8,128)(2,1)S(1)}, bf16[32,8,128]{2,1,0:T(8,128)(2,1)}, u32[]{:S(2)}) copy-start(bf16[32,8,128]{2,1,0:T(8,128)(2,1)} %get-tuple-element.5) | copy-start | bytes 196612
